TPU v7x, 128 devices: a whole 4x4x4 slice. The times are simulated.
128 devices in a mesh: segment: 4 (over y), blk: 32 (over z, x, core).
Axes of the slice: x: 4, y: 4, z: 4, core: 2. Of those that a mesh axis runs over, the one named last changes fastest.
Arguments:
- echoes: bfloat16 [4, 2048, 128, 512], P('segment', 'blk'), may hold values from -6 to 6
- train_blocks: int32 [4, 256, 6], P('segment', 'blk'), may hold values from 0 to 63, as said below
- hard_bins: int32 [4, 256], P('segment', 'blk'), may hold values 0 or 1
- owner_map: int32 [256], replicated, may hold values from 0 to 255, each once
- code_phase: float32 [64], replicated, may hold values from -3.140625 to 3.140625
Outputs:
- returns: bfloat16 [4, 256, 2048, 256], P('segment', 'blk')
Inputs may be any that keep to these rules, and one draw needn't show every extreme that they name: `train_blocks`: each row lists 6 different training blocks.
All inputs are finite; a program needn't handle non-finite values. No bound on the sum of `hard_bins` on one device may be relied on, other than what follows from the above.
Results may differ from a plain program's by a relative error of at most 0.0086.
Values may be sent and summed in bfloat16 or wider, within the bound.
No kernel may reach another device: no remote copies, remote signals or barrier semaphores. Data moves between devices by JAX's collectives and lax.ppermute only.
A program may use at most 128 MiB of HBM per device.

v0:
```python
import math

import jax
import jax.numpy as jnp
from jax import lax
from jax.sharding import PartitionSpec as P

CH = 128
BEAMS = 128
RB = 32
NTR_EASY = 3
NS_STEPS = 12
CBLK = 128


decay_rate = 0.7
diag_load = 0.1
highest = lax.Precision.HIGHEST


def passed_along(x, axis, by):
    peers = lax.axis_size(axis)
    pairs = [(i, i + by) for i in range(peers) if 0 <= i + by < peers]
    return lax.ppermute(x, axis, pairs)


def doppler_table(owner_map, pulse_count):
    pulse_index = jnp.arange(pulse_count, dtype=jnp.int32)
    phase_steps = pulse_index[:, None] * owner_map[None, :] % pulse_count
    angles = phase_steps.astype(jnp.float32) * (2.0 * math.pi / pulse_count)
    cosine = jnp.cos(angles) / math.sqrt(pulse_count)
    sine_part = jnp.sin(angles) / math.sqrt(pulse_count)
    real_rows = jnp.stack([cosine, -sine_part], axis=1)
    imag_rows = jnp.stack([sine_part, cosine], axis=1)
    return jnp.concatenate([real_rows, imag_rows], axis=0).astype(jnp.bfloat16)


def covariance_half(spectra, blocks, hard, block_len, easy_count):
    bin_count, range_count, row_width = spectra.shape
    channels = row_width // 2
    listed = blocks.shape[1]
    blocked = spectra.reshape(bin_count, range_count // block_len, block_len, row_width)
    chosen = jnp.take_along_axis(blocked, blocks[:, :, None, None], axis=1)
    keep_mask = (jnp.arange(listed, dtype=jnp.int32)[None, :] < easy_count) | (hard[:, None] == 1)
    weighted = chosen * keep_mask[:, :, None, None].astype(jnp.bfloat16)
    train_rows = chosen.reshape(bin_count, listed * block_len, row_width)
    weighted = weighted.reshape(bin_count, listed * block_len, row_width)
    real_part = train_rows[..., :channels]
    imag_part = train_rows[..., channels:]
    left_side = jnp.concatenate(
        [train_rows, jnp.concatenate([imag_part, -real_part], axis=-1)], axis=1
    )
    right_side = jnp.concatenate([weighted[..., :channels], weighted[..., channels:]], axis=1)
    gram_sum = jnp.einsum("nsf,nsg->nfg", left_side, right_side, preferred_element_type=jnp.float32)
    row_count = jnp.where(hard == 1, listed * block_len, easy_count * block_len).astype(jnp.float32)
    return gram_sum / row_count[:, None, None]


def steering(channels, beams):
    channel_index = jnp.arange(channels, dtype=jnp.int32)
    beam_index = jnp.arange(beams, dtype=jnp.int32)
    phase_steps = channel_index[:, None] * (2 * beam_index[None, :] - beams) % (2 * beams)
    angles = phase_steps.astype(jnp.float32) * (math.pi / beams)
    return (jnp.cos(angles) / math.sqrt(channels), jnp.sin(angles) / math.sqrt(channels))


def complex_product(first_re, first_im, second_re, second_im):

    def matmul(first, second):
        return jnp.einsum("nij,njk->nik", first, second, precision=highest)

    return (
        matmul(first_re, second_re) - matmul(first_im, second_im),
        matmul(first_re, second_im) + matmul(first_im, second_re),
    )


def beam_weights(cov_half, steer_re, steer_im, steps):
    channels = cov_half.shape[2]
    identity = jnp.eye(channels, dtype=jnp.float32)
    cov_re = cov_half[:, :channels] + diag_load * identity
    cov_im = cov_half[:, channels:]
    trace_value = jnp.trace(cov_re, axis1=1, axis2=2)
    start_re = identity[None] / trace_value[:, None, None]
    start_im = jnp.zeros_like(start_re)

    def newton(step_index, inverse_pair):
        inverse_re, inverse_im = inverse_pair
        middle_re, middle_im = complex_product(cov_re, cov_im, inverse_re, inverse_im)
        return complex_product(inverse_re, inverse_im, 2.0 * identity - middle_re, -middle_im)

    inverse_re, inverse_im = lax.fori_loop(0, steps, newton, (start_re, start_im))

    def apply(matrix, table):
        return jnp.einsum("nij,jb->nib", matrix, table, precision=highest)

    vec_re = apply(inverse_re, steer_re) - apply(inverse_im, steer_im)
    vec_im = apply(inverse_re, steer_im) + apply(inverse_im, steer_re)
    beam_gain = jnp.sum(steer_re * vec_re + steer_im * vec_im, axis=1)
    weight_re = vec_re / beam_gain[:, None, :]
    weight_im = vec_im / beam_gain[:, None, :]
    upper_rows = jnp.concatenate([weight_re, -weight_im], axis=2)
    lower_rows = jnp.concatenate([weight_im, weight_re], axis=2)
    return jnp.concatenate([upper_rows, lower_rows], axis=1).astype(jnp.bfloat16)


def compression_table(code_phase, block_len):
    length = code_phase.shape[0]
    input_pos = jnp.arange(2 * block_len, dtype=jnp.int32)[:, None]
    output_pos = jnp.arange(block_len, dtype=jnp.int32)[None, :]
    lag_index = input_pos - output_pos
    onehot = (lag_index[:, :, None] == jnp.arange(length, dtype=jnp.int32)[None, None, :]).astype(
        jnp.float32
    )
    code_table = jnp.stack([jnp.cos(code_phase), jnp.sin(code_phase)]) / math.sqrt(length)
    table = jnp.einsum("qpl,kl->qkp", onehot, code_table, precision=highest)
    return table.astype(jnp.bfloat16)


def compress(formed, table, block_len):
    bin_count, range_count, row_width = formed.shape
    beam_half = row_width // 2
    blocks = formed.reshape(bin_count, range_count // block_len, block_len, row_width)
    next_blocks = jnp.concatenate([blocks[:, 1:], jnp.zeros_like(blocks[:, :1])], axis=1)
    paired = jnp.concatenate([blocks, next_blocks], axis=2)
    mixed_terms = jnp.einsum("nbqe,qkp->nbkpe", paired, table, preferred_element_type=jnp.float32)
    result_re = mixed_terms[:, :, 0, :, :beam_half] + mixed_terms[:, :, 1, :, beam_half:]
    result_im = mixed_terms[:, :, 0, :, beam_half:] - mixed_terms[:, :, 1, :, :beam_half]
    joined = jnp.concatenate([result_re, result_im], axis=-1)
    return joined.reshape(bin_count, range_count, row_width).astype(jnp.bfloat16)


def local(echoes, train_blocks, hard_bins, owner_map, code_phase):
    samples = echoes[0]
    range_local, channels, double_pulses = samples.shape
    dft_table = doppler_table(owner_map, double_pulses // 2)
    spectra = jnp.einsum("rcp,pkj->jrkc", samples, dft_table, preferred_element_type=jnp.float32)
    spectra = spectra.astype(jnp.bfloat16).reshape(dft_table.shape[2], range_local, 2 * channels)
    owned = lax.all_to_all(spectra, "blk", split_axis=0, concat_axis=1, tiled=True)
    partial_cov = covariance_half(owned, train_blocks[0], hard_bins[0], RB, NTR_EASY)
    carried = jnp.zeros_like(partial_cov)
    for passes in range(lax.axis_size("segment") - 1):
        carried = passed_along(decay_rate * carried + partial_cov, "segment", 1)
    steer_re, steer_im = steering(CH, BEAMS)
    weights = beam_weights(carried, steer_re, steer_im, NS_STEPS)
    formed = jnp.einsum("nrf,nfe->nre", owned, weights, preferred_element_type=jnp.float32).astype(
        jnp.bfloat16
    )
    comp_table = compression_table(code_phase, CBLK)
    return compress(formed, comp_table, CBLK)[None]


def solution(mesh):
    in_specs = (
        P("segment", "blk", None, None),
        P("segment", "blk", None),
        P("segment", "blk"),
        P(),
        P(),
    )
    out_specs = P("segment", "blk", None, None)
    return jax.shard_map(local, mesh=mesh, in_specs=in_specs, out_specs=out_specs, check_vma=False)
```

profile of v0, /device:TPU:50, one launch (start us, length us, event | category | flops | bytes accessed | tf_op | source)
XLA Modules:
  0.0 396.7 jit_solution(18213756322256300456)
XLA Ops:
  0.0 1.8 negate_convert_fusion.1
  1.8 10.1 %convert_bitcast_fusion = bf16[256,64,2,128]{0,3,1,2:T(8,128)(2,1)} fusion(bf16[1,64,128,512]{3,2,1,0:T(8,128)(2,1)} %param.7, bf16[256,1,256]{2,0,1:T(8,128)(2,1)S(1)} %get-tuple-element.98, bf16[256,1,256]{2,0,1:T(8,128)(2,1)S(1)} %get-tuple-element.97, bf16[256,1,256]{2,0,1:T(8,128)(2,1)S(1)} %get-tuple-element.96), kind=kOutput, calls=%fused_computation.28 | convolution fusion | flops 4301258752 | bytes 17170432 | tf_op jit(solution)/shard_map/rcp,pkj->jrkc/dot_general | solution.py:137
  11.9 7.7 %copy.92 = bf16[256,64,2,128]{0,3,2,1:T(8,128)(2,1)} copy(bf16[256,64,2,128]{0,3,1,2:T(8,128)(2,1)} %convert_bitcast_fusion) | data formatting | bytes 16777216 | tf_op jit(solution)/shard_map/convert_element_type | solution.py:138
  19.6 12.1 %copy.93 = bf16[256,64,256]{2,1,0:T(8,128)(2,1)} copy(bf16[256,64,256]{0,2,1:T(8,128)(2,1)} %bitcast.126) | data formatting | bytes 16777216 | tf_op jit(solution)/shard_map/reshape | solution.py:138
  31.8 8.2 %all-to-all-start = ((bf16[256,64,256]{2,1,0:T(8,128)(2,1)}), bf16[256,64,256]{2,1,0:T(8,128)(2,1)}, u32[]{:S(2)}, u32[]{:S(2)}) async-start(bf16[256,64,256]{2,1,0:T(8,128)(2,1)} %copy.93), calls=%async_computation | async-start | bytes 16777216 | tf_op jit(solution)/shard_map/all_to_all | solution.py:139
  40.7 98.3 %all-to-all-done = bf16[256,64,256]{2,1,0:T(8,128)(2,1)} async-done(((bf16[256,64,256]{2,1,0:T(8,128)(2,1)}), bf16[256,64,256]{2,1,0:T(8,128)(2,1)}, u32[]{:S(2)}, u32[]{:S(2)}) %all-to-all-start) | async-done | bytes 8388640 | tf_op jit(solution)/shard_map/all_to_all | solution.py:139
  139.0 8.4 %copy.94 = bf16[8,32,64,256]{3,2,1,0:T(8,128)(2,1)} copy(bf16[8,32,64,256]{3,2,0,1:T(8,128)(2,1)} %bitcast.12) | data formatting | bytes 16777216 | tf_op jit(solution)/shard_map/all_to_all | solution.py:139
  147.5 4.2 %gather_fusion = bf16[48,32,256]{2,1,0:T(8,128)(2,1)S(1)} fusion(bf16[8,64,32,256]{3,2,1,0:T(8,128)(2,1)} %bitcast.129, s32[48]{0:T(128)S(1)} %reshape.400), kind=kCustom, calls=%fused_computation | custom fusion | bytes 1573248 | tf_op jit(solution)/shard_map/jit(take_along_axis)/gather | solution.py:43
  153.2 3.2 collective-permute-start
  156.4 24.6 %collective-permute-done = f32[8,256,128]{2,1,0:T(8,128)S(1)} collective-permute-done((f32[8,256,128]{2,1,0:T(8,128)S(1)}, f32[8,256,128]{2,1,0:T(8,128)S(1)}, u32[]{:S(2)}, u32[]{:S(2)}) %collective-permute-start) | collective-permute-done | bytes 1048608 | tf_op jit(solution)/shard_map/ppermute | solution.py:24
  181.1 3.2 collective-permute-start.1
  184.4 23.8 %collective-permute-done.1 = f32[8,256,128]{2,1,0:T(8,128)S(1)} collective-permute-done((f32[8,256,128]{2,1,0:T(8,128)S(1)}, f32[8,256,128]{2,1,0:T(8,128)S(1)}, u32[]{:S(2)}, u32[]{:S(2)}) %collective-permute-start.1) | collective-permute-done | bytes 1048608 | tf_op jit(solution)/shard_map/ppermute | solution.py:24
  208.3 3.4 collective-permute-start.2
  211.8 2.6 fusion.30
  214.8 19.7 %collective-permute-done.2 = f32[8,256,128]{2,1,0:T(8,128)S(1)} collective-permute-done((f32[8,256,128]{2,1,0:T(8,128)S(1)}, f32[8,256,128]{2,1,0:T(8,128)S(1)}, u32[]{:S(2)}, u32[]{:S(2)}) %collective-permute-start.2) | collective-permute-done | bytes 1048608 | tf_op jit(solution)/shard_map/ppermute | solution.py:24
  234.9 108.3 %while.13 = (s32[]{:T(128)}, f32[8,128,128]{1,2,0:T(8,128)S(1)}, f32[8,128,128]{1,2,0:T(8,128)S(1)}, f32[8,128,128]{2,1,0:T(8,128)S(1)}, f32[8,128,128]{2,1,0:T(8,128)S(1)}, /*index=5*/s32[]{:T(128)}) while((s32[]{:T(128)}, f32[8,128,128]{1,2,0:T(8,128)S(1)}, f32[8,128,128]{1,2,0:T(8,128)S(1)}, f32[8,128,128]{2,1,0:T(8,128)S(1)}, ...), condition=%wide.region_2.3_spmd.clone, body=%wide.region_1.2_spmd.clone.sunk | while | flops 1611431936 | bytes 15859781 | solution.py:92
  234.9 1.2 fusion.181
  244.0 1.2 fusion.181
  247.4 1.2 fusion.177
  256.4 1.2 fusion.177
  262.0 1.2 fusion.181
  271.0 1.2 fusion.181
  283.4 1.2 fusion.177
  289.0 1.2 fusion.181
  298.0 1.2 fusion.181
  310.5 1.2 fusion.177
  316.0 1.2 fusion.181
  347.5 9.0 %convolution_convert_fusion = bf16[8,2048,256]{2,1,0:T(8,128)(2,1)} fusion(bf16[8,2048,256]{2,1,0:T(8,128)(2,1)} %bitcast.130, bf16[8,128,128]{1,2,0:T(8,128)(2,1)S(1)} %get-tuple-element.95, bf16[8,128,128]{1,2,0:T(8,128)(2,1)S(1)} %get-tuple-element.94, bf16[8,128,128]{1,2,0:T(8,128)(2,1)S(1)} %get-tuple-element.93), kind=kOutput, calls=%fused_computation.31 | convolution fusion | flops 2155872256 | bytes 17563648 | tf_op jit(solution)/shard_map/nrf,nfe->nre/dot_general | solution.py:146
  356.5 4.2 %slice.52 = bf16[8,15,128,256]{3,2,1,0:T(8,128)(2,1)S(1)} slice(bf16[8,16,128,256]{3,2,1,0:T(8,128)(2,1)} %bitcast.131), slice={[0:8], [1:16], [0:128], [0:256]} | slice | bytes 15728640 | tf_op jit(solution)/shard_map/slice | solution.py:124
  360.7 14.8 %convolution_bitcast_fusion = f32[8,16,2,128,256]{4,3,1,0,2:T(8,128)} fusion(bf16[8,15,128,256]{3,2,1,0:T(8,128)(2,1)S(1)} %slice.52, bf16[8,16,128,256]{3,2,1,0:T(8,128)(2,1)} %bitcast.132, bf16[256,2,128,1,1]{2,1,0,4,3:T(2,128)(2,1)S(1)} %fusion.30), kind=kOutput, calls=%fused_computation.14 | convolution fusion | flops 4345298944 | bytes 49938432 | tf_op jit(solution)/shard_map/nbqe,qkp->nbkpe/dot_general | solution.py:126
  375.4 14.8 %fusion.15 = (bf16[8,16,1,128,128]{4,3,1,0,2:T(8,128)(2,1)S(1)}, bf16[8,16,1,128,128]{4,3,1,0,2:T(8,128)(2,1)}) fusion(f32[8,16,2,128,256]{4,3,1,0,2:T(8,128)} %convolution_bitcast_fusion), kind=kLoop, calls=%fused_computation.23 | loop fusion | flops 8388608 | bytes 41943040 | tf_op jit(solution)/shard_map/convert.3
  390.3 6.5 %pad_maximum_fusion = bf16[1,8,2048,256]{3,2,1,0:T(8,128)(2,1)} fusion(bf16[1,8,2048,128]{3,2,1,0:T(8,128)(2,1)} %bitcast.128, bf16[1,8,2048,128]{3,2,1,0:T(8,128)(2,1)S(1)} %bitcast.127), kind=kLoop, calls=%fused_computation.25 | loop fusion | flops 16777216 | bytes 16777216 | tf_op jit(solution)/shard_map/concatenate | solution.py:129
  (149 shorter events, 101.5 us)
Async XLA Ops:
  31.8 8.2 %copy-start = (s32[1,8,6]{1,0,2:T(1,128)S(1)}, s32[1,8,6]{1,0,2:T(1,128)}, u32[]{:S(2)}) copy-start(s32[1,8,6]{1,0,2:T(1,128)} %param.8) | copy-start | bytes 580
  31.8 8.7 %copy-start.1 = (s32[1,8]{1,0:T(1,128)S(1)}, s32[1,8]{1,0:T(1,128)}, u32[]{:S(2)}) copy-start(s32[1,8]{1,0:T(1,128)} %param.9) | copy-start | bytes 100
  31.8 107.3 %all-to-all-start = ((bf16[256,64,256]{2,1,0:T(8,128)(2,1)}), bf16[256,64,256]{2,1,0:T(8,128)(2,1)}, u32[]{:S(2)}, u32[]{:S(2)}) async-start(bf16[256,64,256]{2,1,0:T(8,128)(2,1)} %copy.93), calls=%async_computation | async-start | bytes 16777216 | tf_op jit(solution)/shard_map/all_to_all | solution.py:139
  152.4 59.3 %copy-start.2 = (f32[64]{0:T(128)S(1)}, f32[64]{0:T(128)}, u32[]{:S(2)}) copy-start(f32[64]{0:T(128)} %param.11) | copy-start | bytes 772
  153.2 27.8 %collective-permute-start = (f32[8,256,128]{2,1,0:T(8,128)S(1)}, f32[8,256,128]{2,1,0:T(8,128)S(1)}, u32[]{:S(2)}, u32[]{:S(2)}) collective-permute-start(f32[8,256,128]{2,1,0:T(8,128)S(1)} %fusion.38), channel_id=1, source_target_pairs={{0,32},{32,64},{64,96},{1,33},{33,65},{65,97},{2,34},{34,66},{66,9... | collective-permute-start | bytes 3145736 | tf_op jit(solution)/shard_map/ppermute | solution.py:24
  181.1 27.1 %collective-permute-start.1 = (f32[8,256,128]{2,1,0:T(8,128)S(1)}, f32[8,256,128]{2,1,0:T(8,128)S(1)}, u32[]{:S(2)}, u32[]{:S(2)}) collective-permute-start(f32[8,256,128]{2,1,0:T(8,128)S(1)} %multiply_add_fusion.1), channel_id=1, source_target_pairs={{0,32},{32,64},{64,96},{1,33},{33,65},{65,97},{2,34},{34,66},{66,9... | collective-permute-start | bytes 3145736 | tf_op jit(solution)/shard_map/ppermute | solution.py:24
  208.3 26.2 %collective-permute-start.2 = (f32[8,256,128]{2,1,0:T(8,128)S(1)}, f32[8,256,128]{2,1,0:T(8,128)S(1)}, u32[]{:S(2)}, u32[]{:S(2)}) collective-permute-start(f32[8,256,128]{2,1,0:T(8,128)S(1)} %multiply_add_fusion), channel_id=1, source_target_pairs={{0,32},{32,64},{64,96},{1,33},{33,65},{65,97},{2,34},{34,66},{66,9... | collective-permute-start | bytes 3145736 | tf_op jit(solution)/shard_map/ppermute | solution.py:24
where the time goes:
time: 398 us; the launch traced here: 397 us
  waiting for transfers between devices  166 us (42%)
  matrix products  148 us (37%)
  local copies, waits for them, and re-layouts  37.8 us (9%)
  other arithmetic  25.4 us (6%)
  starting transfers between devices  18 us (5%)
    dot_general x96, matrix products, matmul(): return jnp.einsum('nij,njk->nik', first, second, precision=highest)  107 us
    all_to_all x1, waiting for transfers between devices, local(): lax.all_to_all(spectra, 'blk', split_axis=0, concat_axis=1, tiled=True)  98.3 us
    ppermute x3, waiting for transfers between devices, passed_along(): return lax.ppermute(x, axis, pairs)  68 us
    another operation x3, other arithmetic  16.9 us
    dot_general x1, matrix products, compress(): jnp.einsum('nbqe,qkp->nbkpe', paired, table, preferred_element_type=jnp.f...  14.8 us
    reshape x1, local copies, waits for them, and re-layouts, local(): spectra.astype(jnp.bfloat16)  12.1 us
    dot_general x1, matrix products, local(): jnp.einsum('rcp,pkj->jrkc', samples, dft_table, preferred_element_type=jn...  10.1 us
    ppermute x3, starting transfers between devices, passed_along(): return lax.ppermute(x, axis, pairs)  9.75 us
  transfers between devices with their start and end apart: 4, of which 4 were waited for; matrix products, arithmetic and copies ran while one was open for 1% of the time, Pallas kernels for 0%

commit v1 on v0

v1 whole, which is shorter than its diff:
```python
import math

import jax
import jax.numpy as jnp
from jax import lax
from jax.experimental import pallas as pl
from jax.experimental.pallas import tpu as pltpu
from jax.sharding import PartitionSpec as P


CH = 128
BEAMS = 128
RB = 32
NTR_EASY = 3
NS_STEPS = 12
CBLK = 128
CHUNKS = (3, 3, 2)

decay_rate = 0.7
diag_load = 0.1
highest = lax.Precision.HIGHEST
f32 = jnp.float32
bf16 = jnp.bfloat16
MiB = 1 << 20


def params(limit=48):
    return pltpu.CompilerParams(vmem_limit_bytes=limit * MiB)


def shifted(x, by):
    peers = lax.axis_size("segment")
    return lax.ppermute(x, "segment", [(i, i + by) for i in range(peers - by)])


def unit_phasor(index, period):
    eighth = period // 8
    turned = index + eighth
    quadrant = lax.shift_right_logical(turned, int(math.log2(period // 4))) & 3
    rest = (turned & (period // 4 - 1)) - eighth
    x = rest.astype(f32) * (2.0 * math.pi / period)
    x2 = x * x
    sine = x + x * x2 * (-1.0 / 6 + x2 * (1.0 / 120 + x2 * (-1.0 / 5040 + x2 * (1.0 / 362880))))
    cosine = 1.0 + x2 * (
        -0.5 + x2 * (1.0 / 24 + x2 * (-1.0 / 720 + x2 * (1.0 / 40320 - x2 * (1.0 / 3628800))))
    )
    swap = (quadrant & 1) == 1
    c = jnp.where(swap, sine, cosine)
    s = jnp.where(swap, cosine, sine)
    c = jnp.where((quadrant == 1) | (quadrant == 2), -c, c)
    s = jnp.where(quadrant >= 2, -s, s)
    return c, s


def doppler_kernel(map_ref, x_ref, o_ref, table_ref, rows_ref):
    slots, rows, _ = o_ref.shape
    pulses = x_ref.shape[2] // 2

    @pl.when(pl.program_id(0) == 0)
    def _():
        pulse = lax.broadcasted_iota(jnp.int32, (slots, pulses), 1)
        c, s = unit_phasor((pulse * map_ref[...]) & (pulses - 1), pulses)
        c = (c * (1.0 / math.sqrt(pulses))).astype(bf16)
        s = (s * (1.0 / math.sqrt(pulses))).astype(bf16)
        table_ref[:slots, :pulses] = c
        table_ref[:slots, pulses:] = s
        table_ref[slots:, :pulses] = -s
        table_ref[slots:, pulses:] = c

    for pair in range(rows // 2):
        x = x_ref[2 * pair : 2 * pair + 2].reshape(2 * CH, 2 * pulses)
        d = lax.dot_general(
            table_ref[...], x, (((1,), (1,)), ((), ())), preferred_element_type=f32
        )
        for part in range(2):
            for half in range(2):
                rows_ref[part, pl.ds(2 * pair + half, slots, stride=rows), :] = d[
                    part * slots : (part + 1) * slots, half * CH : (half + 1) * CH
                ]
    for part in range(2):
        o_ref[:, :, part * CH : (part + 1) * CH] = (
            rows_ref[part].reshape(slots, rows, CH).astype(bf16)
        )


def doppler(samples, bins):
    range_local, channels, double_pulses = samples.shape
    slots = bins.shape[0]
    step = 16
    return pl.pallas_call(
        doppler_kernel,
        out_shape=pltpu.HBM((slots, range_local, 2 * channels), bf16),
        grid=(range_local // step,),
        in_specs=[
            pl.BlockSpec((slots, 1), lambda i: (0, 0)),
            pl.BlockSpec((step, channels, double_pulses), lambda i: (i, 0, 0)),
        ],
        out_specs=pl.BlockSpec((slots, step, 2 * channels), lambda i: (0, i, 0)),
        scratch_shapes=[
            pltpu.VMEM((2 * slots, double_pulses), bf16),
            pltpu.VMEM((2, slots * step, channels), f32),
        ],
        compiler_params=pltpu.CompilerParams(vmem_limit_bytes=67_043_328),
        name="doppler",
    )(bins, samples)


def make_cov_kernel(first, count, listed):
    def cov_kernel(blocks_ref, hard_ref, y_ref, o_ref, buf, sem):
        per_source = y_ref.shape[2] // RB

        def copy(i, t):
            block = blocks_ref[(first + i) * listed + t]
            source = block // per_source
            row = pl.multiple_of((block % per_source) * RB, RB)
            return pltpu.make_async_copy(
                y_ref.at[source, i, pl.ds(row, RB), :], buf.at[i, t], sem.at[i, t]
            )

        for i in range(count):
            for t in range(listed):
                copy(i, t).start()
        row_of = lax.broadcasted_iota(jnp.int32, (listed * RB, 1), 0)
        f = lax.broadcasted_iota(jnp.int32, (CH, CH), 0)
        g = lax.broadcasted_iota(jnp.int32, (CH, CH), 1)
        for i in range(count):
            for t in range(listed):
                copy(i, t).wait()
            hard = hard_ref[first + i] == 1
            used = jnp.where(hard, listed * RB, NTR_EASY * RB)
            mask = (row_of < used).astype(f32).astype(bf16)
            y = buf[i].reshape(listed * RB, 2 * CH) * mask
            gram = lax.dot_general(y, y, (((0,), (0,)), ((), ())), preferred_element_type=f32)
            re = gram[:CH, :CH] + gram[CH:, CH:]
            im = gram[CH:, :CH] - gram[:CH, CH:]
            o_ref[i] = jnp.where(f <= g, re, im) / used.astype(f32)

    return cov_kernel


def covariance(owned, blocks, hard, first):
    count = owned.shape[1]
    listed = blocks.shape[1]
    smem = pl.BlockSpec(memory_space=pltpu.SMEM)
    return pl.pallas_call(
        make_cov_kernel(first, count, listed),
        out_shape=jax.ShapeDtypeStruct((count, CH, CH), f32),
        in_specs=[smem, smem, pl.BlockSpec(memory_space=pltpu.HBM)],
        out_specs=pl.BlockSpec(memory_space=pltpu.VMEM),
        scratch_shapes=[
            pltpu.VMEM((count, listed, RB, 2 * CH), bf16),
            pltpu.SemaphoreType.DMA((count, listed)),
        ],
        compiler_params=params(),
        name="covariance",
    )(blocks.reshape(-1), hard, owned)


def halves(z):
    high = z.astype(bf16)
    return high, (z - high.astype(f32)).astype(bf16)


def left(z):
    high, low = halves(z)
    return jnp.concatenate([high, low, high], axis=1)


def right(z):
    high, low = halves(z)

    def real_form(x):
        return jnp.concatenate([x, jnp.concatenate([-x[:, CH:], x[:, :CH]], axis=1)], axis=0)

    big = real_form(high)
    return jnp.concatenate([big, big, real_form(low)], axis=0)


def times(a, b):
    return jnp.dot(left(a), right(b), preferred_element_type=f32)


def weights_kernel(c1_ref, c2_ref, c3_ref, o_ref, x_ref, a_ref):
    count = o_ref.shape[0]
    f = lax.broadcasted_iota(jnp.int32, (CH, CH), 0)
    g = lax.broadcasted_iota(jnp.int32, (CH, CH), 1)
    eye = (f == g).astype(f32)
    eye2 = jnp.concatenate([eye, jnp.zeros_like(eye)], axis=1)
    rows = lambda z, k: z[k * CH : (k + 1) * CH]
    for i in range(count):
        packed = c1_ref[i] + decay_rate * c2_ref[i] + (decay_rate * decay_rate) * c3_ref[i]
        flipped = packed.T
        re = jnp.where(f <= g, packed, flipped) + diag_load * eye
        im = jnp.where(f > g, packed, jnp.where(f < g, -flipped, 0.0))
        trace = jnp.sum(jnp.sum(re * eye, axis=1, keepdims=True), axis=0, keepdims=True)
        scale = 1.0 / trace
        a = jnp.concatenate([re, im], axis=1)
        a_ref[i] = right(a)
        e = eye2 - a * scale
        x = (eye2 + e) * scale
        e = times(e, e)
        both = jnp.dot(left(jnp.concatenate([x, e], axis=0)), right(e), preferred_element_type=f32)
        x = x + rows(both, 0)
        x_ref[i] = x + times(x, rows(both, 1))

    def three(_, carry):
        for i in range(count):
            x = x_ref[i]
            e = eye2 - jnp.dot(left(x), a_ref[i], preferred_element_type=f32)
            for _ in range(2):
                both = jnp.dot(
                    left(jnp.concatenate([x, e], axis=0)), right(e), preferred_element_type=f32
                )
                x = x + rows(both, 0)
                e = rows(both, 1)
            x_ref[i] = x + times(x, e)
        return carry

    lax.fori_loop(0, NS_STEPS // 3 - 1, three, 0)
    c, s = unit_phasor((f * (2 * g - BEAMS)) & (2 * BEAMS - 1), 2 * BEAMS)
    steer = jnp.concatenate([c, s], axis=1) * (1.0 / math.sqrt(CH))
    table = right(steer)
    for i in range(count):
        vec = jnp.dot(left(x_ref[i]), table, preferred_element_type=f32)
        both = steer * vec
        gain = jnp.sum(both[:, :BEAMS] + both[:, BEAMS:], axis=0, keepdims=True)
        re = (vec[:, :BEAMS] / gain).astype(bf16)
        im = (vec[:, BEAMS:] / gain).astype(bf16)
        o_ref[i, :CH, :BEAMS] = re
        o_ref[i, :CH, BEAMS:] = -im
        o_ref[i, CH:, :BEAMS] = im
        o_ref[i, CH:, BEAMS:] = re


def beam_weights(c1, c2, c3):
    count = c1.shape[0]
    vmem = pl.BlockSpec(memory_space=pltpu.VMEM)
    return pl.pallas_call(
        weights_kernel,
        out_shape=jax.ShapeDtypeStruct((count, 2 * CH, 2 * BEAMS), bf16),
        in_specs=[vmem] * 3,
        out_specs=vmem,
        scratch_shapes=[
            pltpu.VMEM((count, CH, 2 * CH), f32),
            pltpu.VMEM((count, 6 * CH, 2 * CH), bf16),
        ],
        compiler_params=params(),
        name="weights",
    )(c1, c2, c3)


def compression_table(code_phase, block_len):
    length = code_phase.shape[0]
    input_pos = jnp.arange(2 * block_len, dtype=jnp.int32)[None, :]
    output_pos = jnp.arange(block_len, dtype=jnp.int32)[:, None]
    lag_index = input_pos - output_pos
    onehot = (lag_index[:, :, None] == jnp.arange(length, dtype=jnp.int32)[None, None, :]).astype(
        jnp.float32
    )
    code_table = jnp.stack([jnp.cos(code_phase), jnp.sin(code_phase)]) / math.sqrt(length)
    table = jnp.einsum("pql,kl->kpq", onehot, code_table, precision=highest)
    return table.astype(bf16).reshape(2 * block_len, 2 * block_len)


def compress_kernel(table_ref, y_ref, o_ref):
    per = y_ref.shape[2]
    step = CBLK // per
    sources = y_ref.shape[0]
    half = CH
    for start in range(0, sources, step):
        stop = min(start + 2 * step, sources)
        y = y_ref[start:stop, 0].reshape((stop - start) * per, 2 * half)
        if stop - start < 2 * step:
            y = jnp.concatenate([y, jnp.zeros_like(y)], axis=0)
        m = jnp.dot(table_ref[...], y, preferred_element_type=f32)
        r = pl.ds(start * per, CBLK)
        o_ref[0, r, :half] = (m[:CBLK, :half] + m[CBLK:, half:]).astype(bf16)
        o_ref[0, r, half:] = (m[:CBLK, half:] - m[CBLK:, :half]).astype(bf16)


def compress(owned, table):
    sources, count, per, width = owned.shape
    return pl.pallas_call(
        compress_kernel,
        out_shape=jax.ShapeDtypeStruct((count, sources * per, width), bf16),
        grid=(count,),
        in_specs=[
            pl.BlockSpec(table.shape, lambda i: (0, 0)),
            pl.BlockSpec((sources, 1, per, width), lambda i: (0, i, 0, 0)),
        ],
        out_specs=pl.BlockSpec((1, sources * per, width), lambda i: (i, 0, 0)),
        compiler_params=params(),
        name="compress",
    )(table, owned)


def beams_kernel(w_ref, z_ref, *refs):
    o_ref = refs[-1]
    o_ref[0] = jnp.dot(z_ref[0], w_ref[0], preferred_element_type=f32).astype(bf16)


def form_beams(z, weights, held, bins, first):
    count, rows, width = z.shape
    step = rows // 2
    in_specs = [
        pl.BlockSpec((1, width, weights.shape[2]), lambda i, h: (i, 0, 0)),
        pl.BlockSpec((1, step, width), lambda i, h: (i, h, 0)),
    ]
    operands = [weights, z]
    aliases = {}
    if held is not None:
        in_specs.append(pl.BlockSpec(memory_space=pl.ANY))
        operands.append(held)
        aliases = {2: 0}
    return pl.pallas_call(
        beams_kernel,
        out_shape=jax.ShapeDtypeStruct((bins, rows, weights.shape[2]), bf16),
        grid=(count, 2),
        in_specs=in_specs,
        out_specs=pl.BlockSpec((1, step, weights.shape[2]), lambda i, h: (first + i, h, 0)),
        input_output_aliases=aliases,
        compiler_params=params(),
        name="beams",
    )(*operands)


def chain(echoes, train_blocks, hard_bins, owner_map, code_phase):
    samples = echoes[0]
    blocks, hard = train_blocks[0], hard_bins[0]
    owners = lax.axis_size("blk")
    bins = hard.shape[0]
    slot_bins = owner_map.reshape(owners, bins)
    firsts = [sum(CHUNKS[:i]) for i in range(len(CHUNKS))]
    spectra = []
    for first, count in zip(firsts, CHUNKS):
        chosen = slot_bins[:, first : first + count].reshape(-1, 1)
        spectra.append(doppler(samples, chosen).reshape(owners, count, samples.shape[0], 2 * CH))
    code_phase, spectra[0] = lax.optimization_barrier((code_phase, spectra[0]))
    table = compression_table(code_phase, CBLK)
    owned = []
    for g, sent in enumerate(spectra):
        if g > 0:
            sent, owned[-1] = lax.optimization_barrier((sent, owned[-1]))
        owned.append(lax.all_to_all(sent, "blk", split_axis=0, concat_axis=0, tiled=True))
    result = None
    for first, y in zip(firsts, owned):
        if result is not None:
            y, result = lax.optimization_barrier((y, result))
        cov = covariance(y, blocks, hard, first)
        c1, c2, c3 = shifted(cov, 1), shifted(cov, 2), shifted(cov, 3)
        z = compress(y, table)
        weights = beam_weights(c1, c2, c3)
        result = form_beams(z, weights, result, bins, first)
    return result[None]


def solution(mesh):
    in_specs = (
        P("segment", "blk", None, None),
        P("segment", "blk", None),
        P("segment", "blk"),
        P(),
        P(),
    )
    out_specs = P("segment", "blk", None, None)
    return jax.shard_map(chain, mesh=mesh, in_specs=in_specs, out_specs=out_specs, check_vma=False)
```

time: 398 us -> 202 us (0.51)
  matrix products: 148 us -> 2.64 us
  waiting for transfers between devices: 166 us -> 77.1 us
  Pallas kernels: 0 us -> 78.9 us
  local copies, waits for them, and re-layouts: 37.8 us -> 4.43 us
  other arithmetic: 25.4 us -> 0.01 us
  starting transfers between devices: 18 us -> 37.2 us
    dot_general x105 -> x1, matrix products: 148 us -> 2.64 us  [compression_table(): table = jnp.einsum('pql,kl->kpq', onehot, code_table, precision=highest)]
    pallas_call x0 -> x15, Pallas kernels: none -> 78.9 us  [the longest x3 30 us: beam_weights(): pl.pallas_call(weights_kernel, out_shape=jax.ShapeDtypeStruct((count, 2 *...]
    ppermute x3 -> x9, waiting for transfers between devices: 68 us -> 15.8 us  [shifted(): return lax.ppermute(x, 'segment', [(i, i + by) for i in range(peers - by)])]
    all_to_all x1 -> x3, waiting for transfers between devices: 98.3 us -> 61.4 us  [chain(): lax.all_to_all(sent, 'blk', split_axis=0, concat_axis=0, tiled=True)]
    another operation x3 -> x0, other arithmetic: 16.9 us -> none
    all_to_all x1 -> x3, starting transfers between devices: 8.2 us -> 22.8 us  [chain(): lax.all_to_all(sent, 'blk', split_axis=0, concat_axis=0, tiled=True)]
    reshape x1 -> x4, local copies, waits for them, and re-layouts: 12.1 us -> 2.84 us  [the longest x3 2.08 us: chain(): chosen = slot_bins[:, first:first + count].reshape(-1, 1)]
    all_to_all x1 -> x0, local copies, waits for them, and re-layouts: 8.44 us -> none  [local(): lax.all_to_all(spectra, 'blk', split_axis=0, concat_axis=1, tiled=True)]
  transfers between devices with their start and end apart: 4 -> 12, of which waited for: 4 -> 7; matrix products, arithmetic and copies ran while one was open for 1% -> 2% of each run, Pallas kernels for 0% -> 29%
where the time goes in v1:
time: 202 us; the launch traced here: 201 us
  Pallas kernels  78.9 us (39%)
  waiting for transfers between devices  77.1 us (38%)
  starting transfers between devices  37.2 us (18%)
  local copies, waits for them, and re-layouts  4.43 us (2%)
  matrix products  2.64 us (1%)
    all_to_all x3, waiting for transfers between devices, chain(): lax.all_to_all(sent, 'blk', split_axis=0, concat_axis=0, tiled=True)  61.4 us
    pallas_call x3, Pallas kernels, beam_weights(): pl.pallas_call(weights_kernel, out_shape=jax.ShapeDtypeStruct((count, 2 *...  30 us
    pallas_call x3, Pallas kernels, doppler(): pl.pallas_call(doppler_kernel, out_shape=pltpu.HBM((slots, range_local, 2...  23.6 us
    all_to_all x3, starting transfers between devices, chain(): lax.all_to_all(sent, 'blk', split_axis=0, concat_axis=0, tiled=True)  22.8 us
    ppermute x9, waiting for transfers between devices, shifted(): return lax.ppermute(x, 'segment', [(i, i + by) for i in range(peers - by)])  15.8 us
    ppermute x9, starting transfers between devices, shifted(): return lax.ppermute(x, 'segment', [(i, i + by) for i in range(peers - by)])  14.4 us
    pallas_call x3, Pallas kernels, form_beams(): pl.pallas_call(beams_kernel, out_shape=jax.ShapeDtypeStruct((bins, rows,...  9.76 us
    pallas_call x3, Pallas kernels, compress(): pl.pallas_call(compress_kernel, out_shape=jax.ShapeDtypeStruct((count, so...  9.49 us
  transfers between devices with their start and end apart: 12, of which 7 were waited for; matrix products, arithmetic and copies ran while one was open for 2% of the time, Pallas kernels for 29%

profile of v1, /device:TPU:50, one launch (start us, length us, event | category | flops | bytes accessed | tf_op | source)
XLA Modules:
  0.0 200.6 jit_solution(1144977914181789428)
XLA Ops:
  2.7 8.1 %doppler.5 = bf16[96,64,256]{2,1,0:T(8,128)(2,1)} custom-call(s32[96,1]{1,0:T(8,128)} %reshape.47.map_ref, bf16[64,128,512]{2,1,0:T(8,128)(2,1)} %bitcast.20), custom_call_target="tpu_custom_call" | custom-call | tf_op jit(solution)/shard_map/doppler/pallas_call | solution.py:90
  10.8 8.2 %all-to-all-start = ((bf16[32,3,64,256]{3,2,1,0:T(8,128)(2,1)}), bf16[32,3,64,256]{3,2,1,0:T(8,128)(2,1)}, u32[]{:S(2)}, u32[]{:S(2)}) async-start(bf16[32,3,64,256]{3,2,1,0:T(8,128)(2,1)} %bitcast.24), calls=%async_computation | async-start | bytes 6291456 | tf_op jit(solution)/shard_map/all_to_all | solution.py:344
  19.8 8.0 %doppler.4 = bf16[96,64,256]{2,1,0:T(8,128)(2,1)} custom-call(s32[96,1]{1,0:T(8,128)} %reshape.46.map_ref, bf16[64,128,512]{2,1,0:T(8,128)(2,1)} %bitcast.21), custom_call_target="tpu_custom_call" | custom-call | tf_op jit(solution)/shard_map/doppler/pallas_call | solution.py:90
  27.8 30.4 %all-to-all-done.y_ref = bf16[32,3,64,256]{3,2,1,0:T(8,128)(2,1)} async-done(((bf16[32,3,64,256]{3,2,1,0:T(8,128)(2,1)}), bf16[32,3,64,256]{3,2,1,0:T(8,128)(2,1)}, u32[]{:S(2)}, u32[]{:S(2)}) %all-to-all-start) | async-done | bytes 3145760 | tf_op jit(solution)/shard_map/all_to_all | solution.py:344
  58.2 7.8 %all-to-all-start.1 = ((bf16[32,3,64,256]{3,2,1,0:T(8,128)(2,1)}), bf16[32,3,64,256]{3,2,1,0:T(8,128)(2,1)}, u32[]{:S(2)}, u32[]{:S(2)}) async-start(bf16[32,3,64,256]{3,2,1,0:T(8,128)(2,1)} %bitcast.23), calls=%async_computation.1 | async-start | bytes 6291456 | tf_op jit(solution)/shard_map/all_to_all | solution.py:344
  66.7 7.5 %doppler.3 = bf16[64,64,256]{2,1,0:T(8,128)(2,1)} custom-call(s32[64,1]{1,0:T(8,128)} %reshape.45.map_ref, bf16[64,128,512]{2,1,0:T(8,128)(2,1)} %bitcast.22), custom_call_target="tpu_custom_call" | custom-call | tf_op jit(solution)/shard_map/doppler/pallas_call | solution.py:90
  74.2 30.9 %all-to-all-done.1.y_ref = bf16[32,3,64,256]{3,2,1,0:T(8,128)(2,1)} async-done(((bf16[32,3,64,256]{3,2,1,0:T(8,128)(2,1)}), bf16[32,3,64,256]{3,2,1,0:T(8,128)(2,1)}, u32[]{:S(2)}, u32[]{:S(2)}) %all-to-all-start.1) | async-done | bytes 3145760 | tf_op jit(solution)/shard_map/all_to_all | solution.py:344
  105.2 6.9 %all-to-all-start.2 = ((bf16[32,2,64,256]{3,2,1,0:T(8,128)(2,1)}), bf16[32,2,64,256]{3,2,1,0:T(8,128)(2,1)S(1)}, u32[]{:S(2)}, u32[]{:S(2)}) async-start(bf16[32,2,64,256]{3,2,1,0:T(8,128)(2,1)} %bitcast.25), calls=%async_computation.2 | async-start | bytes 4194304 | tf_op jit(solution)/shard_map/all_to_all | solution.py:344
  112.3 2.3 %covariance.3 = f32[3,128,128]{2,1,0:T(8,128)S(1)} custom-call(s32[48]{0:T(128)S(1)} %reshape_squeeze.2.blocks_ref, s32[8]{0:T(128)S(1)} %bitcast.17, bf16[32,3,64,256]{3,2,1,0:T(8,128)(2,1)} %all-to-all-done.y_ref), custom_call_target="tpu_custom_call" | custom-call | tf_op jit(solution)/shard_map/covariance/pallas_call | solution.py:145
  115.2 1.3 collective-permute-start.1
  116.5 4.0 %collective-permute-start = (f32[3,128,128]{2,1,0:T(8,128)S(1)}, f32[3,128,128]{2,1,0:T(8,128)S(1)}, u32[]{:S(2)}, u32[]{:S(2)}) collective-permute-start(f32[3,128,128]{2,1,0:T(8,128)S(1)} %covariance.3), channel_id=1, source_target_pairs={{0,32},{32,64},{64,96},{1,33},{33,65},{65,97},{2,34},{34,66},{66,9... | collective-permute-start | bytes 589832 | tf_op jit(solution)/shard_map/ppermute | solution.py:33
  120.5 2.6 %fusion.2 = bf16[2,128,256]{2,0,1:T(2,128)(2,1)S(1)} fusion(s32[128,256]{1,0:T(8,128)S(1)} %iota_subtract_fusion, f32[1,64]{1,0:T(1,128)S(1)} %get-tuple-element.28, f32[1,64]{1,0:T(1,128)S(1)} %get-tuple-element.27), kind=kOutput, calls=%fused_computation.3 | convolution fusion | flops 52494592 | bytes 262656 | tf_op jit(solution)/shard_map/pql,kl->kpq/dot_general | solution.py:261
  123.2 3.9 %compress.3.z_ref = bf16[3,2048,256]{2,1,0:T(8,128)(2,1)S(1)} custom-call(bf16[256,256]{1,0:T(8,128)(2,1)S(1)} %bitcast.14, bf16[32,3,64,256]{3,2,1,0:T(8,128)(2,1)} %all-to-all-done.y_ref), custom_call_target="tpu_custom_call" | custom-call | tf_op jit(solution)/shard_map/compress/pallas_call | solution.py:283
  127.2 3.1 %collective-permute-done.c1_ref = f32[3,128,128]{2,1,0:T(8,128)S(1)} collective-permute-done((f32[3,128,128]{2,1,0:T(8,128)S(1)}, f32[3,128,128]{2,1,0:T(8,128)S(1)}, u32[]{:S(2)}, u32[]{:S(2)}) %collective-permute-start) | collective-permute-done | bytes 196640 | tf_op jit(solution)/shard_map/ppermute | solution.py:33
  130.2 11.0 %weights.3.w_ref = bf16[3,256,256]{2,1,0:T(8,128)(2,1)S(1)} custom-call(f32[3,128,128]{2,1,0:T(8,128)S(1)} %collective-permute-done.c1_ref, f32[3,128,128]{2,1,0:T(8,128)S(1)} %collective-permute-done.1.c2_ref, f32[3,128,128]{2,1,0:T(8,128)S(1)} %collective-permute-done.2.c3_ref), custom_call_target="tpu_custom_call" | custom-call | tf_op jit(solution)/shard_map/weights/pallas_call | solution.py:238
  141.3 3.6 %beams.3.refs_0_ = bf16[8,2048,256]{2,1,0:T(8,128)(2,1)} custom-call(bf16[3,256,256]{2,1,0:T(8,128)(2,1)S(1)} %weights.3.w_ref, bf16[3,2048,256]{2,1,0:T(8,128)(2,1)S(1)} %compress.3.z_ref), custom_call_target="tpu_custom_call" | custom-call | tf_op jit(solution)/shard_map/beams/pallas_call | solution.py:315
  144.9 2.3 %covariance.4 = f32[3,128,128]{2,1,0:T(8,128)S(1)} custom-call(s32[48]{0:T(128)S(1)} %reshape_squeeze.2.blocks_ref, s32[8]{0:T(128)S(1)} %bitcast.18, bf16[32,3,64,256]{3,2,1,0:T(8,128)(2,1)} %all-to-all-done.1.y_ref), custom_call_target="tpu_custom_call" | custom-call | tf_op jit(solution)/shard_map/covariance/pallas_call | solution.py:145
  147.8 1.3 collective-permute-start.4
  149.1 2.6 %collective-permute-start.3 = (f32[3,128,128]{2,1,0:T(8,128)S(1)}, f32[3,128,128]{2,1,0:T(8,128)S(1)}, u32[]{:S(2)}, u32[]{:S(2)}) collective-permute-start(f32[3,128,128]{2,1,0:T(8,128)S(1)} %covariance.4), channel_id=1, source_target_pairs={{0,32},{32,64},{64,96},{1,33},{33,65},{65,97},{2,34},{34,66},{66,9... | collective-permute-start | bytes 589832 | tf_op jit(solution)/shard_map/ppermute | solution.py:33
  151.8 3.9 %compress.4.z_ref = bf16[3,2048,256]{2,1,0:T(8,128)(2,1)S(1)} custom-call(bf16[256,256]{1,0:T(8,128)(2,1)S(1)} %bitcast.15, bf16[32,3,64,256]{3,2,1,0:T(8,128)(2,1)} %all-to-all-done.1.y_ref), custom_call_target="tpu_custom_call" | custom-call | tf_op jit(solution)/shard_map/compress/pallas_call | solution.py:283
  155.7 3.3 %collective-permute-done.4.c2_ref = f32[3,128,128]{2,1,0:T(8,128)S(1)} collective-permute-done((f32[3,128,128]{2,1,0:T(8,128)S(1)}, f32[3,128,128]{2,1,0:T(8,128)S(1)}, u32[]{:S(2)}, u32[]{:S(2)}) %collective-permute-start.4) | collective-permute-done | bytes 196640 | tf_op jit(solution)/shard_map/ppermute | solution.py:33
  159.1 3.0 %collective-permute-done.3.c1_ref = f32[3,128,128]{2,1,0:T(8,128)S(1)} collective-permute-done((f32[3,128,128]{2,1,0:T(8,128)S(1)}, f32[3,128,128]{2,1,0:T(8,128)S(1)}, u32[]{:S(2)}, u32[]{:S(2)}) %collective-permute-start.3) | collective-permute-done | bytes 196640 | tf_op jit(solution)/shard_map/ppermute | solution.py:33
  162.1 11.0 %weights.4.w_ref = bf16[3,256,256]{2,1,0:T(8,128)(2,1)S(1)} custom-call(f32[3,128,128]{2,1,0:T(8,128)S(1)} %collective-permute-done.3.c1_ref, f32[3,128,128]{2,1,0:T(8,128)S(1)} %collective-permute-done.4.c2_ref, f32[3,128,128]{2,1,0:T(8,128)S(1)} %collective-permute-done.5.c3_ref), custom_call_target="tpu_custom_call" | custom-call | tf_op jit(solution)/shard_map/weights/pallas_call | solution.py:238
  173.1 3.6 %beams.4.refs_0_ = bf16[8,2048,256]{2,1,0:T(8,128)(2,1)} custom-call(bf16[3,256,256]{2,1,0:T(8,128)(2,1)S(1)} %weights.4.w_ref, bf16[3,2048,256]{2,1,0:T(8,128)(2,1)S(1)} %compress.4.z_ref, bf16[8,2048,256]{2,1,0:T(8,128)(2,1)} %beams.3.refs_0_), custom_call_target="tpu_custom_call", output_to_operand_aliasing={{}: (2, {})} | custom-call | tf_op jit(solution)/shard_map/beams/pallas_call | solution.py:315
  176.7 1.6 covariance.5
  179.0 1.3 collective-permute-start.7
  180.3 1.9 collective-permute-start.6
  182.2 1.6 compress.5.z_ref
  183.8 4.9 %collective-permute-done.7.c2_ref = f32[2,128,128]{2,1,0:T(8,128)S(1)} collective-permute-done((f32[2,128,128]{2,1,0:T(8,128)S(1)}, f32[2,128,128]{2,1,0:T(8,128)S(1)}, u32[]{:S(2)}, u32[]{:S(2)}) %collective-permute-start.7) | collective-permute-done | bytes 131104 | tf_op jit(solution)/shard_map/ppermute | solution.py:33
  188.7 1.4 collective-permute-done.6.c1_ref
  190.2 7.9 %weights.5.w_ref = bf16[2,256,256]{2,1,0:T(8,128)(2,1)S(1)} custom-call(f32[2,128,128]{2,1,0:T(8,128)S(1)} %collective-permute-done.6.c1_ref, f32[2,128,128]{2,1,0:T(8,128)S(1)} %collective-permute-done.7.c2_ref, f32[2,128,128]{2,1,0:T(8,128)S(1)} %collective-permute-done.8.c3_ref), custom_call_target="tpu_custom_call" | custom-call | tf_op jit(solution)/shard_map/weights/pallas_call | solution.py:238
  198.1 2.5 %beams.5 = bf16[8,2048,256]{2,1,0:T(8,128)(2,1)} custom-call(bf16[2,256,256]{2,1,0:T(8,128)(2,1)S(1)} %weights.5.w_ref, bf16[2,2048,256]{2,1,0:T(8,128)(2,1)S(1)} %compress.5.z_ref, bf16[8,2048,256]{2,1,0:T(8,128)(2,1)} %beams.4.refs_0_), custom_call_target="tpu_custom_call", output_to_operand_aliasing={{}: (2, {})} | custom-call | tf_op jit(solution)/shard_map/beams/pallas_call | solution.py:315
  (31 shorter events, 6.5 us)
Async XLA Ops:
  0.8 0.6 copy-start.1
  10.8 8.2 %copy-start.3 = (s32[32,3]{1,0:T(8,128)S(1)}, s32[32,3]{1,0:T(8,128)}, u32[]{:S(2)}) copy-start(s32[32,3]{1,0:T(8,128)} %get-tuple-element.26) | copy-start | bytes 1156
  10.8 47.3 %all-to-all-start = ((bf16[32,3,64,256]{3,2,1,0:T(8,128)(2,1)}), bf16[32,3,64,256]{3,2,1,0:T(8,128)(2,1)}, u32[]{:S(2)}, u32[]{:S(2)}) async-start(bf16[32,3,64,256]{3,2,1,0:T(8,128)(2,1)} %bitcast.24), calls=%async_computation | async-start | bytes 6291456 | tf_op jit(solution)/shard_map/all_to_all | solution.py:344
  58.2 7.8 %copy-start.2 = (s32[32,8]{1,0:T(8,128)S(1)}, s32[32,8]{1,0:T(8,128)}, u32[]{:S(2)}) copy-start(s32[32,8]{1,0:T(8,128)} %copy-done.1) | copy-start | bytes 3076
  58.2 47.0 %all-to-all-start.1 = ((bf16[32,3,64,256]{3,2,1,0:T(8,128)(2,1)}), bf16[32,3,64,256]{3,2,1,0:T(8,128)(2,1)}, u32[]{:S(2)}, u32[]{:S(2)}) async-start(bf16[32,3,64,256]{3,2,1,0:T(8,128)(2,1)} %bitcast.23), calls=%async_computation.1 | async-start | bytes 6291456 | tf_op jit(solution)/shard_map/all_to_all | solution.py:344
  74.2 37.8 %copy-start.4 = (s32[1,8,6]{1,0,2:T(1,128)S(1)}, s32[1,8,6]{1,0,2:T(1,128)}, u32[]{:S(2)}) copy-start(s32[1,8,6]{1,0,2:T(1,128)} %param.6) | copy-start | bytes 580
  74.2 38.0 %copy-start.5 = (f32[64]{0:T(128)S(1)}, f32[64]{0:T(128)}, u32[]{:S(2)}) copy-start(f32[64]{0:T(128)} %param.9) | copy-start | bytes 772
  74.2 38.1 %copy-start = (s32[1,8]{1,0:T(1,128)S(1)}, s32[1,8]{1,0:T(1,128)}, u32[]{:S(2)}) copy-start(s32[1,8]{1,0:T(1,128)} %param.7) | copy-start | bytes 100
  105.2 71.6 %all-to-all-start.2 = ((bf16[32,2,64,256]{3,2,1,0:T(8,128)(2,1)}), bf16[32,2,64,256]{3,2,1,0:T(8,128)(2,1)S(1)}, u32[]{:S(2)}, u32[]{:S(2)}) async-start(bf16[32,2,64,256]{3,2,1,0:T(8,128)(2,1)} %bitcast.25), calls=%async_computation.2 | async-start | bytes 4194304 | tf_op jit(solution)/shard_map/all_to_all | solution.py:344
  114.6 12.6 %collective-permute-start.2 = (f32[3,128,128]{2,1,0:T(8,128)S(1)}, f32[3,128,128]{2,1,0:T(8,128)S(1)}, u32[]{:S(2)}, u32[]{:S(2)}) collective-permute-start(f32[3,128,128]{2,1,0:T(8,128)S(1)} %covariance.3), channel_id=1, source_target_pairs={{0,96},{1,97},{2,98},{3,99},{4,100},{5,101},{6,102},{7,103},{8,104... | collective-permute-start | bytes 589832 | tf_op jit(solution)/shard_map/ppermute | solution.py:33
  115.2 11.9 %collective-permute-start.1 = (f32[3,128,128]{2,1,0:T(8,128)S(1)}, f32[3,128,128]{2,1,0:T(8,128)S(1)}, u32[]{:S(2)}, u32[]{:S(2)}) collective-permute-start(f32[3,128,128]{2,1,0:T(8,128)S(1)} %covariance.3), channel_id=1, source_target_pairs={{0,64},{32,96},{1,65},{33,97},{2,66},{34,98},{3,67},{35,99},{4,68}... | collective-permute-start | bytes 589832 | tf_op jit(solution)/shard_map/ppermute | solution.py:33
  116.5 13.7 %collective-permute-start = (f32[3,128,128]{2,1,0:T(8,128)S(1)}, f32[3,128,128]{2,1,0:T(8,128)S(1)}, u32[]{:S(2)}, u32[]{:S(2)}) collective-permute-start(f32[3,128,128]{2,1,0:T(8,128)S(1)} %covariance.3), channel_id=1, source_target_pairs={{0,32},{32,64},{64,96},{1,33},{33,65},{65,97},{2,34},{34,66},{66,9... | collective-permute-start | bytes 589832 | tf_op jit(solution)/shard_map/ppermute | solution.py:33
  147.1 8.5 %collective-permute-start.5 = (f32[3,128,128]{2,1,0:T(8,128)S(1)}, f32[3,128,128]{2,1,0:T(8,128)S(1)}, u32[]{:S(2)}, u32[]{:S(2)}) collective-permute-start(f32[3,128,128]{2,1,0:T(8,128)S(1)} %covariance.4), channel_id=1, source_target_pairs={{0,96},{1,97},{2,98},{3,99},{4,100},{5,101},{6,102},{7,103},{8,104... | collective-permute-start | bytes 589832 | tf_op jit(solution)/shard_map/ppermute | solution.py:33
  147.8 11.2 %collective-permute-start.4 = (f32[3,128,128]{2,1,0:T(8,128)S(1)}, f32[3,128,128]{2,1,0:T(8,128)S(1)}, u32[]{:S(2)}, u32[]{:S(2)}) collective-permute-start(f32[3,128,128]{2,1,0:T(8,128)S(1)} %covariance.4), channel_id=1, source_target_pairs={{0,64},{32,96},{1,65},{33,97},{2,66},{34,98},{3,67},{35,99},{4,68}... | collective-permute-start | bytes 589832 | tf_op jit(solution)/shard_map/ppermute | solution.py:33
  149.1 12.9 %collective-permute-start.3 = (f32[3,128,128]{2,1,0:T(8,128)S(1)}, f32[3,128,128]{2,1,0:T(8,128)S(1)}, u32[]{:S(2)}, u32[]{:S(2)}) collective-permute-start(f32[3,128,128]{2,1,0:T(8,128)S(1)} %covariance.4), channel_id=1, source_target_pairs={{0,32},{32,64},{64,96},{1,33},{33,65},{65,97},{2,34},{34,66},{66,9... | collective-permute-start | bytes 589832 | tf_op jit(solution)/shard_map/ppermute | solution.py:33
  178.3 5.5 %collective-permute-start.8 = (f32[2,128,128]{2,1,0:T(8,128)S(1)}, f32[2,128,128]{2,1,0:T(8,128)S(1)}, u32[]{:S(2)}, u32[]{:S(2)}) collective-permute-start(f32[2,128,128]{2,1,0:T(8,128)S(1)} %covariance.5), channel_id=1, source_target_pairs={{0,96},{1,97},{2,98},{3,99},{4,100},{5,101},{6,102},{7,103},{8,104... | collective-permute-start | bytes 393224 | tf_op jit(solution)/shard_map/ppermute | solution.py:33
  179.0 9.8 %collective-permute-start.7 = (f32[2,128,128]{2,1,0:T(8,128)S(1)}, f32[2,128,128]{2,1,0:T(8,128)S(1)}, u32[]{:S(2)}, u32[]{:S(2)}) collective-permute-start(f32[2,128,128]{2,1,0:T(8,128)S(1)} %covariance.5), channel_id=1, source_target_pairs={{0,64},{32,96},{1,65},{33,97},{2,66},{34,98},{3,67},{35,99},{4,68}... | collective-permute-start | bytes 393224 | tf_op jit(solution)/shard_map/ppermute | solution.py:33
  180.3 9.9 %collective-permute-start.6 = (f32[2,128,128]{2,1,0:T(8,128)S(1)}, f32[2,128,128]{2,1,0:T(8,128)S(1)}, u32[]{:S(2)}, u32[]{:S(2)}) collective-permute-start(f32[2,128,128]{2,1,0:T(8,128)S(1)} %covariance.5), channel_id=1, source_target_pairs={{0,32},{32,64},{64,96},{1,33},{33,65},{65,97},{2,34},{34,66},{66,9... | collective-permute-start | bytes 393224 | tf_op jit(solution)/shard_map/ppermute | solution.py:33

commit v2 on v1

--- a/solution.py
+++ b/solution.py
@@ -30,7 +30,7 @@
 
 def shifted(x, by):
     peers = lax.axis_size("segment")
-    return lax.ppermute(x, "segment", [(i, i + by) for i in range(peers - by)])
+    return lax.ppermute(x, "segment", [(i, (i + by) % peers) for i in range(peers)])
 
 
 def unit_phasor(index, period):
@@ -52,14 +52,34 @@
     return c, s
 
 
-def doppler_kernel(map_ref, x_ref, o_ref, table_ref, rows_ref):
-    slots, rows, _ = o_ref.shape
-    pulses = x_ref.shape[2] // 2
-
-    @pl.when(pl.program_id(0) == 0)
-    def _():
+def make_doppler_kernel(owners, first, count):
+    def doppler_kernel(map_ref, x_hbm, o_hbm, x_ref, table_ref, rows_ref, o_ref, in_sem, out_sem):
+        slots = owners * count
+        total = map_ref.shape[1]
+        bins = total // owners
+        pulses = x_ref.shape[2] // 2
+        groups, _, rows, _ = o_ref.shape
+        pitch = rows_ref.shape[1] // slots
+        loads = in_sem.shape[0]
+        per_load = x_ref.shape[0] // loads
+
+        def load(i):
+            piece = pl.ds(i * per_load, per_load)
+            return pltpu.make_async_copy(x_hbm.at[piece], x_ref.at[piece], in_sem.at[i])
+
+        def save(i):
+            piece = o_hbm.at[:, pl.ds(i * rows, rows), :]
+            return pltpu.make_async_copy(o_ref.at[i], piece, out_sem.at[i])
+
+        for i in range(loads):
+            load(i).start()
+        slot = lax.broadcasted_iota(jnp.int32, (slots, total), 1)
+        row = lax.broadcasted_iota(jnp.int32, (slots, total), 0)
+        place = slot % bins - first
+        mine = (place >= 0) & (place < count) & (slot // bins * count + place == row)
+        chosen = jnp.sum(jnp.where(mine, map_ref[...].astype(f32), 0.0), axis=1, keepdims=True)
         pulse = lax.broadcasted_iota(jnp.int32, (slots, pulses), 1)
-        c, s = unit_phasor((pulse * map_ref[...]) & (pulses - 1), pulses)
+        c, s = unit_phasor((pulse * chosen.astype(jnp.int32)) & (pulses - 1), pulses)
         c = (c * (1.0 / math.sqrt(pulses))).astype(bf16)
         s = (s * (1.0 / math.sqrt(pulses))).astype(bf16)
         table_ref[:slots, :pulses] = c
@@ -67,42 +87,57 @@
         table_ref[slots:, :pulses] = -s
         table_ref[slots:, pulses:] = c
 
-    for pair in range(rows // 2):
-        x = x_ref[2 * pair : 2 * pair + 2].reshape(2 * CH, 2 * pulses)
-        d = lax.dot_general(
-            table_ref[...], x, (((1,), (1,)), ((), ())), preferred_element_type=f32
-        )
-        for part in range(2):
-            for half in range(2):
-                rows_ref[part, pl.ds(2 * pair + half, slots, stride=rows), :] = d[
-                    part * slots : (part + 1) * slots, half * CH : (half + 1) * CH
-                ]
-    for part in range(2):
-        o_ref[:, :, part * CH : (part + 1) * CH] = (
-            rows_ref[part].reshape(slots, rows, CH).astype(bf16)
-        )
-
-
-def doppler(samples, bins):
+        def group(i, carry):
+            for j in range(loads // groups):
+                load(i * (loads // groups) + j).wait()
+            for pair in range(rows // 2):
+                x = x_ref[pl.ds(i * rows + 2 * pair, 2)].reshape(2 * CH, 2 * pulses)
+                d = lax.dot_general(
+                    table_ref[...], x, (((1,), (1,)), ((), ())), preferred_element_type=f32
+                )
+                for part in range(2):
+                    for half in range(2):
+                        rows_ref[part, pl.ds(2 * pair + half, slots, stride=pitch), :] = d[
+                            part * slots : (part + 1) * slots, half * CH : (half + 1) * CH
+                        ]
+            for part in range(2):
+                o_ref[i, :, :, part * CH : (part + 1) * CH] = (
+                    rows_ref[part].reshape(slots, pitch, CH)[:, :rows].astype(bf16)
+                )
+            save(i).start()
+            return carry
+
+        lax.fori_loop(0, groups, group, 0)
+        for i in range(groups):
+            save(i).wait()
+
+    return doppler_kernel
+
+
+def doppler(samples, owner_map, owners, first, count):
     range_local, channels, double_pulses = samples.shape
-    slots = bins.shape[0]
-    step = 16
+    slots = owners * count
+    rows, pitch, loads = 16, 24, 8
+    groups = range_local // rows
     return pl.pallas_call(
-        doppler_kernel,
+        make_doppler_kernel(owners, first, count),
         out_shape=pltpu.HBM((slots, range_local, 2 * channels), bf16),
-        grid=(range_local // step,),
         in_specs=[
-            pl.BlockSpec((slots, 1), lambda i: (0, 0)),
-            pl.BlockSpec((step, channels, double_pulses), lambda i: (i, 0, 0)),
+            pl.BlockSpec(memory_space=pltpu.VMEM),
+            pl.BlockSpec(memory_space=pl.ANY),
         ],
-        out_specs=pl.BlockSpec((slots, step, 2 * channels), lambda i: (0, i, 0)),
+        out_specs=pl.BlockSpec(memory_space=pl.ANY),
         scratch_shapes=[
+            pltpu.VMEM(samples.shape, bf16),
             pltpu.VMEM((2 * slots, double_pulses), bf16),
-            pltpu.VMEM((2, slots * step, channels), f32),
+            pltpu.VMEM((2, slots * pitch, channels), f32),
+            pltpu.VMEM((groups, slots, rows, 2 * channels), bf16),
+            pltpu.SemaphoreType.DMA((loads,)),
+            pltpu.SemaphoreType.DMA((groups,)),
         ],
         compiler_params=pltpu.CompilerParams(vmem_limit_bytes=67_043_328),
         name="doppler",
-    )(bins, samples)
+    )(owner_map.reshape(1, -1), samples)
 
 
 def make_cov_kernel(first, count, listed):
@@ -110,7 +145,7 @@
         per_source = y_ref.shape[2] // RB
 
         def copy(i, t):
-            block = blocks_ref[(first + i) * listed + t]
+            block = blocks_ref[first + i, t]
             source = block // per_source
             row = pl.multiple_of((block % per_source) * RB, RB)
             return pltpu.make_async_copy(
@@ -153,7 +188,7 @@
         ],
         compiler_params=params(),
         name="covariance",
-    )(blocks.reshape(-1), hard, owned)
+    )(blocks, hard, owned)
 
 
 def halves(z):
@@ -187,8 +222,10 @@
     eye = (f == g).astype(f32)
     eye2 = jnp.concatenate([eye, jnp.zeros_like(eye)], axis=1)
     rows = lambda z, k: z[k * CH : (k + 1) * CH]
+    segment = lax.axis_index("segment")
+    decay = [jnp.where(segment > n, decay_rate**n, 0.0) for n in range(3)]
     for i in range(count):
-        packed = c1_ref[i] + decay_rate * c2_ref[i] + (decay_rate * decay_rate) * c3_ref[i]
+        packed = decay[0] * c1_ref[i] + decay[1] * c2_ref[i] + decay[2] * c3_ref[i]
         flipped = packed.T
         re = jnp.where(f <= g, packed, flipped) + diag_load * eye
         im = jnp.where(f > g, packed, jnp.where(f < g, -flipped, 0.0))
@@ -329,12 +366,11 @@
     blocks, hard = train_blocks[0], hard_bins[0]
     owners = lax.axis_size("blk")
     bins = hard.shape[0]
-    slot_bins = owner_map.reshape(owners, bins)
     firsts = [sum(CHUNKS[:i]) for i in range(len(CHUNKS))]
     spectra = []
     for first, count in zip(firsts, CHUNKS):
-        chosen = slot_bins[:, first : first + count].reshape(-1, 1)
-        spectra.append(doppler(samples, chosen).reshape(owners, count, samples.shape[0], 2 * CH))
+        sent = doppler(samples, owner_map, owners, first, count)
+        spectra.append(sent.reshape(owners, count, samples.shape[0], 2 * CH))
     code_phase, spectra[0] = lax.optimization_barrier((code_phase, spectra[0]))
     table = compression_table(code_phase, CBLK)
     owned = []
@@ -347,7 +383,7 @@
         if result is not None:
             y, result = lax.optimization_barrier((y, result))
         cov = covariance(y, blocks, hard, first)
-        c1, c2, c3 = shifted(cov, 1), shifted(cov, 2), shifted(cov, 3)
+        c3, c1, c2 = shifted(cov, 3), shifted(cov, 1), shifted(cov, 2)
         z = compress(y, table)
         weights = beam_weights(c1, c2, c3)
         result = form_beams(z, weights, result, bins, first)

time: 202 us -> 194 us (0.960)
  the two profiles are of different devices: /device:TPU:50 before, /device:TPU:1 now
where the time goes in v2:
time: 194 us; the launch traced here: 193 us
  waiting for transfers between devices  84.3 us (43%)
  Pallas kernels  76.4 us (39%)
  starting transfers between devices  29.4 us (15%)
  matrix products  2.64 us (1%)
    all_to_all x3, waiting for transfers between devices, chain(): lax.all_to_all(sent, 'blk', split_axis=0, concat_axis=0, tiled=True)  66 us
    pallas_call x3, Pallas kernels, beam_weights(): pl.pallas_call(weights_kernel, out_shape=jax.ShapeDtypeStruct((count, 2 *...  30 us
    all_to_all x3, starting transfers between devices, chain(): lax.all_to_all(sent, 'blk', split_axis=0, concat_axis=0, tiled=True)  22.5 us
    pallas_call x3, Pallas kernels, doppler(): pl.pallas_call(make_doppler_kernel(owners, first, count), out_shape=pltpu...  20.9 us
    ppermute x9, waiting for transfers between devices, shifted(): lax.ppermute(x, 'segment', [(i, (i + by) % peers) for i in range(peers)])  18.3 us
    pallas_call x3, Pallas kernels, form_beams(): pl.pallas_call(beams_kernel, out_shape=jax.ShapeDtypeStruct((bins, rows,...  9.76 us
    pallas_call x3, Pallas kernels, compress(): pl.pallas_call(compress_kernel, out_shape=jax.ShapeDtypeStruct((count, so...  9.51 us
    ppermute x9, starting transfers between devices, shifted(): lax.ppermute(x, 'segment', [(i, (i + by) % peers) for i in range(peers)])  6.91 us
  transfers between devices with their start and end apart: 12, of which 10 were waited for; matrix products, arithmetic and copies ran while one was open for 1% of the time, Pallas kernels for 30%

profile of v2, /device:TPU:1, one launch (start us, length us, event | category | flops | bytes accessed | tf_op | source)
XLA Modules:
  0.0 193.1 jit_solution(8134158501858156969)
XLA Ops:
  0.0 7.1 %doppler.5 = bf16[96,64,256]{2,1,0:T(8,128)(2,1)} custom-call(s32[1,256]{1,0:T(1,128)} %bitcast.31, bf16[64,128,512]{2,1,0:T(8,128)(2,1)} %bitcast.25), custom_call_target="tpu_custom_call" | custom-call | tf_op jit(solution)/shard_map/doppler/pallas_call | solution.py:122
  7.1 9.5 %all-to-all-start = ((bf16[32,3,64,256]{3,2,1,0:T(8,128)(2,1)}), bf16[32,3,64,256]{3,2,1,0:T(8,128)(2,1)}, u32[]{:S(2)}, u32[]{:S(2)}) async-start(bf16[32,3,64,256]{3,2,1,0:T(8,128)(2,1)} %bitcast.29), calls=%async_computation | async-start | bytes 6291456 | tf_op jit(solution)/shard_map/all_to_all | solution.py:380
  16.6 7.0 %doppler.4 = bf16[96,64,256]{2,1,0:T(8,128)(2,1)} custom-call(s32[1,256]{1,0:T(1,128)} %bitcast.32, bf16[64,128,512]{2,1,0:T(8,128)(2,1)} %bitcast.26), custom_call_target="tpu_custom_call" | custom-call | tf_op jit(solution)/shard_map/doppler/pallas_call | solution.py:122
  23.6 32.8 %all-to-all-done.y_ref = bf16[32,3,64,256]{3,2,1,0:T(8,128)(2,1)} async-done(((bf16[32,3,64,256]{3,2,1,0:T(8,128)(2,1)}), bf16[32,3,64,256]{3,2,1,0:T(8,128)(2,1)}, u32[]{:S(2)}, u32[]{:S(2)}) %all-to-all-start) | async-done | bytes 3145760 | tf_op jit(solution)/shard_map/all_to_all | solution.py:380
  56.4 6.9 %all-to-all-start.1 = ((bf16[32,3,64,256]{3,2,1,0:T(8,128)(2,1)}), bf16[32,3,64,256]{3,2,1,0:T(8,128)(2,1)}, u32[]{:S(2)}, u32[]{:S(2)}) async-start(bf16[32,3,64,256]{3,2,1,0:T(8,128)(2,1)} %bitcast.28), calls=%async_computation.1 | async-start | bytes 6291456 | tf_op jit(solution)/shard_map/all_to_all | solution.py:380
  63.3 6.7 %doppler.3 = bf16[64,64,256]{2,1,0:T(8,128)(2,1)} custom-call(s32[1,256]{1,0:T(1,128)} %bitcast.33, bf16[64,128,512]{2,1,0:T(8,128)(2,1)} %bitcast.27), custom_call_target="tpu_custom_call" | custom-call | tf_op jit(solution)/shard_map/doppler/pallas_call | solution.py:122
  70.1 33.1 %all-to-all-done.1.y_ref = bf16[32,3,64,256]{3,2,1,0:T(8,128)(2,1)} async-done(((bf16[32,3,64,256]{3,2,1,0:T(8,128)(2,1)}), bf16[32,3,64,256]{3,2,1,0:T(8,128)(2,1)}, u32[]{:S(2)}, u32[]{:S(2)}) %all-to-all-start.1) | async-done | bytes 3145760 | tf_op jit(solution)/shard_map/all_to_all | solution.py:380
  103.3 6.1 %all-to-all-start.2 = ((bf16[32,2,64,256]{3,2,1,0:T(8,128)(2,1)}), bf16[32,2,64,256]{3,2,1,0:T(8,128)(2,1)S(1)}, u32[]{:S(2)}, u32[]{:S(2)}) async-start(bf16[32,2,64,256]{3,2,1,0:T(8,128)(2,1)} %bitcast.30), calls=%async_computation.2 | async-start | bytes 4194304 | tf_op jit(solution)/shard_map/all_to_all | solution.py:380
  109.6 2.3 %covariance.3 = f32[3,128,128]{2,1,0:T(8,128)S(1)} custom-call(s32[8,6]{1,0:T(8,128)S(1)} %bitcast.19, s32[8]{0:T(128)S(1)} %bitcast.22, bf16[32,3,64,256]{3,2,1,0:T(8,128)(2,1)} %all-to-all-done.y_ref), custom_call_target="tpu_custom_call" | custom-call | tf_op jit(solution)/shard_map/covariance/pallas_call | solution.py:180
  111.9 2.8 %collective-permute-start.2 = (f32[3,128,128]{2,1,0:T(8,128)S(1)}, f32[3,128,128]{2,1,0:T(8,128)S(1)}, u32[]{:S(2)}, u32[]{:S(2)}) collective-permute-start(f32[3,128,128]{2,1,0:T(8,128)S(1)} %covariance.3), channel_id=1, source_target_pairs={{0,96},{32,0},{64,32},{96,64},{1,97},{33,1},{65,33},{97,65},{2,98}... | collective-permute-start | bytes 589832 | tf_op jit(solution)/shard_map/ppermute | solution.py:33
  115.1 0.7 collective-permute-start
  115.8 2.6 %fusion.2 = bf16[2,128,256]{2,0,1:T(2,128)(2,1)S(1)} fusion(s32[128,256]{1,0:T(8,128)S(1)} %iota_subtract_fusion, f32[1,64]{1,0:T(1,128)S(1)} %get-tuple-element.26, f32[1,64]{1,0:T(1,128)S(1)} %get-tuple-element.25), kind=kOutput, calls=%fused_computation.3 | convolution fusion | flops 52494592 | bytes 262656 | tf_op jit(solution)/shard_map/pql,kl->kpq/dot_general | solution.py:298
  118.4 3.9 %compress.3.z_ref = bf16[3,2048,256]{2,1,0:T(8,128)(2,1)S(1)} custom-call(bf16[256,256]{1,0:T(8,128)(2,1)S(1)} %bitcast.16, bf16[32,3,64,256]{3,2,1,0:T(8,128)(2,1)} %all-to-all-done.y_ref), custom_call_target="tpu_custom_call" | custom-call | tf_op jit(solution)/shard_map/compress/pallas_call | solution.py:320
  122.7 4.6 %collective-permute-done.c1_ref = f32[3,128,128]{2,1,0:T(8,128)S(1)} collective-permute-done((f32[3,128,128]{2,1,0:T(8,128)S(1)}, f32[3,128,128]{2,1,0:T(8,128)S(1)}, u32[]{:S(2)}, u32[]{:S(2)}) %collective-permute-start) | collective-permute-done | bytes 196640 | tf_op jit(solution)/shard_map/ppermute | solution.py:33
  127.3 11.0 %weights.3.w_ref = bf16[3,256,256]{2,1,0:T(8,128)(2,1)S(1)} custom-call(f32[3,128,128]{2,1,0:T(8,128)S(1)} %collective-permute-done.c1_ref, f32[3,128,128]{2,1,0:T(8,128)S(1)} %collective-permute-done.1.c2_ref, f32[3,128,128]{2,1,0:T(8,128)S(1)} %collective-permute-done.2.c3_ref), custom_call_target="tpu_custom_call" | custom-call | tf_op jit(solution)/shard_map/weights/pallas_call | solution.py:275
  138.3 3.6 %beams.3.refs_0_ = bf16[8,2048,256]{2,1,0:T(8,128)(2,1)} custom-call(bf16[3,256,256]{2,1,0:T(8,128)(2,1)S(1)} %weights.3.w_ref, bf16[3,2048,256]{2,1,0:T(8,128)(2,1)S(1)} %compress.3.z_ref), custom_call_target="tpu_custom_call" | custom-call | tf_op jit(solution)/shard_map/beams/pallas_call | solution.py:352
  141.9 2.3 %covariance.4 = f32[3,128,128]{2,1,0:T(8,128)S(1)} custom-call(s32[8,6]{1,0:T(8,128)S(1)} %bitcast.20, s32[8]{0:T(128)S(1)} %bitcast.23, bf16[32,3,64,256]{3,2,1,0:T(8,128)(2,1)} %all-to-all-done.1.y_ref), custom_call_target="tpu_custom_call" | custom-call | tf_op jit(solution)/shard_map/covariance/pallas_call | solution.py:180
  144.8 1.0 collective-permute-start.3
  145.8 3.9 %compress.4.z_ref = bf16[3,2048,256]{2,1,0:T(8,128)(2,1)S(1)} custom-call(bf16[256,256]{1,0:T(8,128)(2,1)S(1)} %bitcast.17, bf16[32,3,64,256]{3,2,1,0:T(8,128)(2,1)} %all-to-all-done.1.y_ref), custom_call_target="tpu_custom_call" | custom-call | tf_op jit(solution)/shard_map/compress/pallas_call | solution.py:320
  149.7 0.6 collective-permute-done.5.c3_ref
  150.3 1.1 collective-permute-done.4.c2_ref
  151.4 5.5 %collective-permute-done.3.c1_ref = f32[3,128,128]{2,1,0:T(8,128)S(1)} collective-permute-done((f32[3,128,128]{2,1,0:T(8,128)S(1)}, f32[3,128,128]{2,1,0:T(8,128)S(1)}, u32[]{:S(2)}, u32[]{:S(2)}) %collective-permute-start.3) | collective-permute-done | bytes 196640 | tf_op jit(solution)/shard_map/ppermute | solution.py:33
  157.0 11.0 %weights.4.w_ref = bf16[3,256,256]{2,1,0:T(8,128)(2,1)S(1)} custom-call(f32[3,128,128]{2,1,0:T(8,128)S(1)} %collective-permute-done.3.c1_ref, f32[3,128,128]{2,1,0:T(8,128)S(1)} %collective-permute-done.4.c2_ref, f32[3,128,128]{2,1,0:T(8,128)S(1)} %collective-permute-done.5.c3_ref), custom_call_target="tpu_custom_call" | custom-call | tf_op jit(solution)/shard_map/weights/pallas_call | solution.py:275
  168.0 3.6 %beams.4.refs_0_ = bf16[8,2048,256]{2,1,0:T(8,128)(2,1)} custom-call(bf16[3,256,256]{2,1,0:T(8,128)(2,1)S(1)} %weights.4.w_ref, bf16[3,2048,256]{2,1,0:T(8,128)(2,1)S(1)} %compress.4.z_ref, bf16[8,2048,256]{2,1,0:T(8,128)(2,1)} %beams.3.refs_0_), custom_call_target="tpu_custom_call", output_to_operand_aliasing={{}: (2, {})} | custom-call | tf_op jit(solution)/shard_map/beams/pallas_call | solution.py:352
  171.6 1.6 covariance.5
  173.7 1.0 collective-permute-start.6
  174.8 1.6 compress.5.z_ref
  176.4 1.5 collective-permute-done.8.c3_ref
  177.9 0.9 collective-permute-done.7.c2_ref
  178.8 3.9 %collective-permute-done.6.c1_ref = f32[2,128,128]{2,1,0:T(8,128)S(1)} collective-permute-done((f32[2,128,128]{2,1,0:T(8,128)S(1)}, f32[2,128,128]{2,1,0:T(8,128)S(1)}, u32[]{:S(2)}, u32[]{:S(2)}) %collective-permute-start.6) | collective-permute-done | bytes 131104 | tf_op jit(solution)/shard_map/ppermute | solution.py:33
  182.7 7.9 %weights.5.w_ref = bf16[2,256,256]{2,1,0:T(8,128)(2,1)S(1)} custom-call(f32[2,128,128]{2,1,0:T(8,128)S(1)} %collective-permute-done.6.c1_ref, f32[2,128,128]{2,1,0:T(8,128)S(1)} %collective-permute-done.7.c2_ref, f32[2,128,128]{2,1,0:T(8,128)S(1)} %collective-permute-done.8.c3_ref), custom_call_target="tpu_custom_call" | custom-call | tf_op jit(solution)/shard_map/weights/pallas_call | solution.py:275
  190.6 2.5 %beams.5 = bf16[8,2048,256]{2,1,0:T(8,128)(2,1)} custom-call(bf16[2,256,256]{2,1,0:T(8,128)(2,1)S(1)} %weights.5.w_ref, bf16[2,2048,256]{2,1,0:T(8,128)(2,1)S(1)} %compress.5.z_ref, bf16[8,2048,256]{2,1,0:T(8,128)(2,1)} %beams.4.refs_0_), custom_call_target="tpu_custom_call", output_to_operand_aliasing={{}: (2, {})} | custom-call | tf_op jit(solution)/shard_map/beams/pallas_call | solution.py:352
  (18 shorter events, 1.8 us)
Async XLA Ops:
  7.1 49.3 %all-to-all-start = ((bf16[32,3,64,256]{3,2,1,0:T(8,128)(2,1)}), bf16[32,3,64,256]{3,2,1,0:T(8,128)(2,1)}, u32[]{:S(2)}, u32[]{:S(2)}) async-start(bf16[32,3,64,256]{3,2,1,0:T(8,128)(2,1)} %bitcast.29), calls=%async_computation | async-start | bytes 6291456 | tf_op jit(solution)/shard_map/all_to_all | solution.py:380
  56.4 46.8 %all-to-all-start.1 = ((bf16[32,3,64,256]{3,2,1,0:T(8,128)(2,1)}), bf16[32,3,64,256]{3,2,1,0:T(8,128)(2,1)}, u32[]{:S(2)}, u32[]{:S(2)}) async-start(bf16[32,3,64,256]{3,2,1,0:T(8,128)(2,1)} %bitcast.28), calls=%async_computation.1 | async-start | bytes 6291456 | tf_op jit(solution)/shard_map/all_to_all | solution.py:380
  70.1 39.3 %copy-start.1 = (s32[1,8,6]{1,0,2:T(1,128)S(1)}, s32[1,8,6]{1,0,2:T(1,128)}, u32[]{:S(2)}) copy-start(s32[1,8,6]{1,0,2:T(1,128)} %param.6) | copy-start | bytes 580
  70.1 39.4 %copy-start.2 = (f32[64]{0:T(128)S(1)}, f32[64]{0:T(128)}, u32[]{:S(2)}) copy-start(f32[64]{0:T(128)} %param.9) | copy-start | bytes 772
  70.1 39.5 %copy-start = (s32[1,8]{1,0:T(1,128)S(1)}, s32[1,8]{1,0:T(1,128)}, u32[]{:S(2)}) copy-start(s32[1,8]{1,0:T(1,128)} %param.7) | copy-start | bytes 100
  103.3 68.3 %all-to-all-start.2 = ((bf16[32,2,64,256]{3,2,1,0:T(8,128)(2,1)}), bf16[32,2,64,256]{3,2,1,0:T(8,128)(2,1)S(1)}, u32[]{:S(2)}, u32[]{:S(2)}) async-start(bf16[32,2,64,256]{3,2,1,0:T(8,128)(2,1)} %bitcast.30), calls=%async_computation.2 | async-start | bytes 4194304 | tf_op jit(solution)/shard_map/all_to_all | solution.py:380
  111.9 10.8 %collective-permute-start.2 = (f32[3,128,128]{2,1,0:T(8,128)S(1)}, f32[3,128,128]{2,1,0:T(8,128)S(1)}, u32[]{:S(2)}, u32[]{:S(2)}) collective-permute-start(f32[3,128,128]{2,1,0:T(8,128)S(1)} %covariance.3), channel_id=1, source_target_pairs={{0,96},{32,0},{64,32},{96,64},{1,97},{33,1},{65,33},{97,65},{2,98}... | collective-permute-start | bytes 589832 | tf_op jit(solution)/shard_map/ppermute | solution.py:33
  114.7 8.0 %collective-permute-start.1 = (f32[3,128,128]{2,1,0:T(8,128)S(1)}, f32[3,128,128]{2,1,0:T(8,128)S(1)}, u32[]{:S(2)}, u32[]{:S(2)}) collective-permute-start(f32[3,128,128]{2,1,0:T(8,128)S(1)} %covariance.3), channel_id=1, source_target_pairs={{0,64},{32,96},{64,0},{96,32},{1,65},{33,97},{65,1},{97,33},{2,66}... | collective-permute-start | bytes 589832 | tf_op jit(solution)/shard_map/ppermute | solution.py:33
  115.1 12.2 %collective-permute-start = (f32[3,128,128]{2,1,0:T(8,128)S(1)}, f32[3,128,128]{2,1,0:T(8,128)S(1)}, u32[]{:S(2)}, u32[]{:S(2)}) collective-permute-start(f32[3,128,128]{2,1,0:T(8,128)S(1)} %covariance.3), channel_id=1, source_target_pairs={{0,32},{32,64},{64,96},{96,0},{1,33},{33,65},{65,97},{97,1},{2,34}... | collective-permute-start | bytes 589832 | tf_op jit(solution)/shard_map/ppermute | solution.py:33
  144.2 6.0 %collective-permute-start.5 = (f32[3,128,128]{2,1,0:T(8,128)S(1)}, f32[3,128,128]{2,1,0:T(8,128)S(1)}, u32[]{:S(2)}, u32[]{:S(2)}) collective-permute-start(f32[3,128,128]{2,1,0:T(8,128)S(1)} %covariance.4), channel_id=1, source_target_pairs={{0,96},{32,0},{64,32},{96,64},{1,97},{33,1},{65,33},{97,65},{2,98}... | collective-permute-start | bytes 589832 | tf_op jit(solution)/shard_map/ppermute | solution.py:33
  144.3 7.1 %collective-permute-start.4 = (f32[3,128,128]{2,1,0:T(8,128)S(1)}, f32[3,128,128]{2,1,0:T(8,128)S(1)}, u32[]{:S(2)}, u32[]{:S(2)}) collective-permute-start(f32[3,128,128]{2,1,0:T(8,128)S(1)} %covariance.4), channel_id=1, source_target_pairs={{0,64},{32,96},{64,0},{96,32},{1,65},{33,97},{65,1},{97,33},{2,66}... | collective-permute-start | bytes 589832 | tf_op jit(solution)/shard_map/ppermute | solution.py:33
  144.8 12.2 %collective-permute-start.3 = (f32[3,128,128]{2,1,0:T(8,128)S(1)}, f32[3,128,128]{2,1,0:T(8,128)S(1)}, u32[]{:S(2)}, u32[]{:S(2)}) collective-permute-start(f32[3,128,128]{2,1,0:T(8,128)S(1)} %covariance.4), channel_id=1, source_target_pairs={{0,32},{32,64},{64,96},{96,0},{1,33},{33,65},{65,97},{97,1},{2,34}... | collective-permute-start | bytes 589832 | tf_op jit(solution)/shard_map/ppermute | solution.py:33
  173.2 4.6 %collective-permute-start.8 = (f32[2,128,128]{2,1,0:T(8,128)S(1)}, f32[2,128,128]{2,1,0:T(8,128)S(1)}, u32[]{:S(2)}, u32[]{:S(2)}) collective-permute-start(f32[2,128,128]{2,1,0:T(8,128)S(1)} %covariance.5), channel_id=1, source_target_pairs={{0,96},{32,0},{64,32},{96,64},{1,97},{33,1},{65,33},{97,65},{2,98}... | collective-permute-start | bytes 393224 | tf_op jit(solution)/shard_map/ppermute | solution.py:33
  173.3 5.5 %collective-permute-start.7 = (f32[2,128,128]{2,1,0:T(8,128)S(1)}, f32[2,128,128]{2,1,0:T(8,128)S(1)}, u32[]{:S(2)}, u32[]{:S(2)}) collective-permute-start(f32[2,128,128]{2,1,0:T(8,128)S(1)} %covariance.5), channel_id=1, source_target_pairs={{0,64},{32,96},{64,0},{96,32},{1,65},{33,97},{65,1},{97,33},{2,66}... | collective-permute-start | bytes 393224 | tf_op jit(solution)/shard_map/ppermute | solution.py:33
  173.7 8.9 %collective-permute-start.6 = (f32[2,128,128]{2,1,0:T(8,128)S(1)}, f32[2,128,128]{2,1,0:T(8,128)S(1)}, u32[]{:S(2)}, u32[]{:S(2)}) collective-permute-start(f32[2,128,128]{2,1,0:T(8,128)S(1)} %covariance.5), channel_id=1, source_target_pairs={{0,32},{32,64},{64,96},{96,0},{1,33},{33,65},{65,97},{97,1},{2,34}... | collective-permute-start | bytes 393224 | tf_op jit(solution)/shard_map/ppermute | solution.py:33

commit v3 on v2

--- a/solution.py
+++ b/solution.py
@@ -14,7 +14,7 @@
 NTR_EASY = 3
 NS_STEPS = 12
 CBLK = 128
-CHUNKS = (3, 3, 2)
+CHUNKS = (6, 2)
 
 decay_rate = 0.7
 diag_load = 0.1
@@ -161,14 +161,21 @@
         for i in range(count):
             for t in range(listed):
                 copy(i, t).wait()
-            hard = hard_ref[first + i] == 1
-            used = jnp.where(hard, listed * RB, NTR_EASY * RB)
-            mask = (row_of < used).astype(f32).astype(bf16)
-            y = buf[i].reshape(listed * RB, 2 * CH) * mask
-            gram = lax.dot_general(y, y, (((0,), (0,)), ((), ())), preferred_element_type=f32)
-            re = gram[:CH, :CH] + gram[CH:, CH:]
-            im = gram[CH:, :CH] - gram[:CH, CH:]
-            o_ref[i] = jnp.where(f <= g, re, im) / used.astype(f32)
+        used = [
+            jnp.where(hard_ref[first + i] == 1, listed * RB, NTR_EASY * RB) for i in range(count)
+        ]
+        rows = [
+            buf[i].reshape(listed * RB, 2 * CH) * (row_of < used[i]).astype(f32).astype(bf16)
+            for i in range(count)
+        ]
+        grams = [
+            lax.dot_general(y, y, (((0,), (0,)), ((), ())), preferred_element_type=f32)
+            for y in rows
+        ]
+        for i in range(count):
+            re = grams[i][:CH, :CH] + grams[i][CH:, CH:]
+            im = grams[i][CH:, :CH] - grams[i][:CH, CH:]
+            o_ref[i] = jnp.where(f <= g, re, im) / used[i].astype(f32)
 
     return cov_kernel
 
@@ -186,7 +193,7 @@
             pltpu.VMEM((count, listed, RB, 2 * CH), bf16),
             pltpu.SemaphoreType.DMA((count, listed)),
         ],
-        compiler_params=params(),
+        compiler_params=params(16),
         name="covariance",
     )(blocks, hard, owned)
 
@@ -211,79 +218,85 @@
     return jnp.concatenate([big, big, real_form(low)], axis=0)
 
 
-def times(a, b):
-    return jnp.dot(left(a), right(b), preferred_element_type=f32)
-
-
-def weights_kernel(c1_ref, c2_ref, c3_ref, o_ref, x_ref, a_ref):
+def product(a, b):
+    return jnp.dot(a, b, preferred_element_type=f32)
+
+
+def weights_kernel(c1_ref, c3_ref, *refs):
+    *c2_refs, o_ref = refs
+    twos = [(ref, j) for ref in c2_refs for j in range(ref.shape[0])]
     count = o_ref.shape[0]
+    bins = range(count)
     f = lax.broadcasted_iota(jnp.int32, (CH, CH), 0)
     g = lax.broadcasted_iota(jnp.int32, (CH, CH), 1)
     eye = (f == g).astype(f32)
     eye2 = jnp.concatenate([eye, jnp.zeros_like(eye)], axis=1)
-    rows = lambda z, k: z[k * CH : (k + 1) * CH]
     segment = lax.axis_index("segment")
     decay = [jnp.where(segment > n, decay_rate**n, 0.0) for n in range(3)]
-    for i in range(count):
-        packed = decay[0] * c1_ref[i] + decay[1] * c2_ref[i] + decay[2] * c3_ref[i]
+    a, x, e = [], [], []
+    for i in bins:
+        ref, j = twos[i]
+        packed = decay[0] * c1_ref[i] + decay[1] * ref[j] + decay[2] * c3_ref[i]
         flipped = packed.T
         re = jnp.where(f <= g, packed, flipped) + diag_load * eye
         im = jnp.where(f > g, packed, jnp.where(f < g, -flipped, 0.0))
-        trace = jnp.sum(jnp.sum(re * eye, axis=1, keepdims=True), axis=0, keepdims=True)
-        scale = 1.0 / trace
-        a = jnp.concatenate([re, im], axis=1)
-        a_ref[i] = right(a)
-        e = eye2 - a * scale
-        x = (eye2 + e) * scale
-        e = times(e, e)
-        both = jnp.dot(left(jnp.concatenate([x, e], axis=0)), right(e), preferred_element_type=f32)
-        x = x + rows(both, 0)
-        x_ref[i] = x + times(x, rows(both, 1))
-
-    def three(_, carry):
-        for i in range(count):
-            x = x_ref[i]
-            e = eye2 - jnp.dot(left(x), a_ref[i], preferred_element_type=f32)
-            for _ in range(2):
-                both = jnp.dot(
-                    left(jnp.concatenate([x, e], axis=0)), right(e), preferred_element_type=f32
-                )
-                x = x + rows(both, 0)
-                e = rows(both, 1)
-            x_ref[i] = x + times(x, e)
-        return carry
-
-    lax.fori_loop(0, NS_STEPS // 3 - 1, three, 0)
+        scale = 1.0 / jnp.sum(jnp.sum(re * eye, axis=1, keepdims=True), axis=0, keepdims=True)
+        loaded = jnp.concatenate([re, im], axis=1)
+        a.append(right(loaded))
+        e.append(eye2 - loaded * scale)
+        x.append((eye2 + e[i]) * scale)
+
+    def both(x, e):
+        return left(jnp.concatenate([x, e], axis=0))
+
+    for turn in range(NS_STEPS // 3):
+        if turn == 0:
+            e = [product(left(e[i]), right(e[i])) for i in bins]
+        else:
+            e = [eye2 - product(left(x[i]), a[i]) for i in bins]
+        for _ in range(1 if turn == 0 else 2):
+            m = [product(both(x[i], e[i]), right(e[i])) for i in bins]
+            x = [x[i] + m[i][:CH] for i in bins]
+            e = [m[i][CH:] for i in bins]
+        x = [x[i] + product(left(x[i]), right(e[i])) for i in bins]
+
     c, s = unit_phasor((f * (2 * g - BEAMS)) & (2 * BEAMS - 1), 2 * BEAMS)
     steer = jnp.concatenate([c, s], axis=1) * (1.0 / math.sqrt(CH))
     table = right(steer)
-    for i in range(count):
-        vec = jnp.dot(left(x_ref[i]), table, preferred_element_type=f32)
-        both = steer * vec
-        gain = jnp.sum(both[:, :BEAMS] + both[:, BEAMS:], axis=0, keepdims=True)
-        re = (vec[:, :BEAMS] / gain).astype(bf16)
-        im = (vec[:, BEAMS:] / gain).astype(bf16)
+    vec = [product(left(x[i]), table) for i in bins]
+    for i in bins:
+        inner = steer * vec[i]
+        gain = jnp.sum(inner[:, :BEAMS] + inner[:, BEAMS:], axis=0, keepdims=True)
+        re = (vec[i][:, :BEAMS] / gain).astype(bf16)
+        im = (vec[i][:, BEAMS:] / gain).astype(bf16)
         o_ref[i, :CH, :BEAMS] = re
         o_ref[i, :CH, BEAMS:] = -im
         o_ref[i, CH:, :BEAMS] = im
         o_ref[i, CH:, BEAMS:] = re
 
 
-def beam_weights(c1, c2, c3):
+def beam_weights(c1, c3, twos):
     count = c1.shape[0]
     vmem = pl.BlockSpec(memory_space=pltpu.VMEM)
     return pl.pallas_call(
         weights_kernel,
         out_shape=jax.ShapeDtypeStruct((count, 2 * CH, 2 * BEAMS), bf16),
-        in_specs=[vmem] * 3,
+        in_specs=[vmem] * (2 + len(twos)),
         out_specs=vmem,
-        scratch_shapes=[
-            pltpu.VMEM((count, CH, 2 * CH), f32),
-            pltpu.VMEM((count, 6 * CH, 2 * CH), bf16),
-        ],
-        compiler_params=params(),
+        compiler_params=params(32),
         name="weights",
-    )(c1, c2, c3)
+    )(c1, c3, *twos)
+
+
+def earlier(cov):
+    count = cov.shape[0]
+    if count < 4:
+        c3, c1, c2 = shifted(cov, 3), shifted(cov, 1), shifted(cov, 2)
+        return c1, c3, [c2]
+    c1 = shifted(cov, 1)
+    c3 = shifted(cov, 3)
+    split = count // 2
+    return c1, c3, [shifted(c1[:split], 1), shifted(c3[split:], 3)]
 
 
 def compression_table(code_phase, block_len):
@@ -299,64 +312,100 @@
     return table.astype(bf16).reshape(2 * block_len, 2 * block_len)
 
 
-def compress_kernel(table_ref, y_ref, o_ref):
-    per = y_ref.shape[2]
+def compress_kernel(table_ref, y_hbm, z_hbm, y_ref, z_ref, in_sem, out_sem):
+    count, sources, per, _ = y_ref.shape
     step = CBLK // per
-    sources = y_ref.shape[0]
     half = CH
-    for start in range(0, sources, step):
-        stop = min(start + 2 * step, sources)
-        y = y_ref[start:stop, 0].reshape((stop - start) * per, 2 * half)
-        if stop - start < 2 * step:
-            y = jnp.concatenate([y, jnp.zeros_like(y)], axis=0)
-        m = jnp.dot(table_ref[...], y, preferred_element_type=f32)
-        r = pl.ds(start * per, CBLK)
-        o_ref[0, r, :half] = (m[:CBLK, :half] + m[CBLK:, half:]).astype(bf16)
-        o_ref[0, r, half:] = (m[:CBLK, half:] - m[CBLK:, :half]).astype(bf16)
+
+    def load(i):
+        return pltpu.make_async_copy(y_hbm.at[:, i], y_ref.at[i], in_sem.at[i])
+
+    def save(i):
+        return pltpu.make_async_copy(z_ref.at[i], z_hbm.at[i], out_sem.at[i])
+
+    for i in range(count):
+        load(i).start()
+    for i in range(count):
+        load(i).wait()
+        for start in range(0, sources, step):
+            stop = min(start + 2 * step, sources)
+            y = y_ref[i, start:stop].reshape((stop - start) * per, 2 * half)
+            m = jnp.dot(table_ref[:, : y.shape[0]], y, preferred_element_type=f32)
+            r = pl.ds(start * per, CBLK)
+            z_ref[i, r, :half] = (m[:CBLK, :half] + m[CBLK:, half:]).astype(bf16)
+            z_ref[i, r, half:] = (m[:CBLK, half:] - m[CBLK:, :half]).astype(bf16)
+        save(i).start()
+    for i in range(count):
+        save(i).wait()
 
 
 def compress(owned, table):
     sources, count, per, width = owned.shape
+    anywhere = pl.BlockSpec(memory_space=pl.ANY)
+    place = pltpu.HBM if count > 3 else jax.ShapeDtypeStruct
     return pl.pallas_call(
         compress_kernel,
-        out_shape=jax.ShapeDtypeStruct((count, sources * per, width), bf16),
-        grid=(count,),
-        in_specs=[
-            pl.BlockSpec(table.shape, lambda i: (0, 0)),
-            pl.BlockSpec((sources, 1, per, width), lambda i: (0, i, 0, 0)),
+        out_shape=place((count, sources * per, width), bf16),
+        in_specs=[pl.BlockSpec(memory_space=pltpu.VMEM), anywhere],
+        out_specs=anywhere,
+        scratch_shapes=[
+            pltpu.VMEM((count, sources, per, width), bf16),
+            pltpu.VMEM((count, sources * per, width), bf16),
+            pltpu.SemaphoreType.DMA((count,)),
+            pltpu.SemaphoreType.DMA((count,)),
         ],
-        out_specs=pl.BlockSpec((1, sources * per, width), lambda i: (i, 0, 0)),
-        compiler_params=params(),
+        compiler_params=params(32),
         name="compress",
     )(table, owned)
 
 
-def beams_kernel(w_ref, z_ref, *refs):
-    o_ref = refs[-1]
-    o_ref[0] = jnp.dot(z_ref[0], w_ref[0], preferred_element_type=f32).astype(bf16)
+def make_beams_kernel(first):
+    def beams_kernel(w_ref, z_hbm, *refs):
+        *_, o_hbm, z_ref, o_ref, in_sem, out_sem = refs
+        count = z_ref.shape[0]
+
+        def load(i):
+            return pltpu.make_async_copy(z_hbm.at[i], z_ref.at[i], in_sem.at[i])
+
+        def save(i):
+            return pltpu.make_async_copy(o_ref.at[i], o_hbm.at[first + i], out_sem.at[i])
+
+        for i in range(count):
+            load(i).start()
+        for i in range(count):
+            load(i).wait()
+            o_ref[i] = jnp.dot(z_ref[i], w_ref[i], preferred_element_type=f32).astype(bf16)
+            save(i).start()
+        for i in range(count):
+            save(i).wait()
+
+    return beams_kernel
 
 
 def form_beams(z, weights, held, bins, first):
-    count, rows, width = z.shape
-    step = rows // 2
-    in_specs = [
-        pl.BlockSpec((1, width, weights.shape[2]), lambda i, h: (i, 0, 0)),
-        pl.BlockSpec((1, step, width), lambda i, h: (i, h, 0)),
-    ]
+    count, rows, _ = z.shape
+    width = weights.shape[2]
+    anywhere = pl.BlockSpec(memory_space=pl.ANY)
+    in_specs = [pl.BlockSpec(memory_space=pltpu.VMEM), anywhere]
     operands = [weights, z]
     aliases = {}
     if held is not None:
-        in_specs.append(pl.BlockSpec(memory_space=pl.ANY))
+        in_specs.append(anywhere)
         operands.append(held)
         aliases = {2: 0}
     return pl.pallas_call(
-        beams_kernel,
-        out_shape=jax.ShapeDtypeStruct((bins, rows, weights.shape[2]), bf16),
-        grid=(count, 2),
+        make_beams_kernel(first),
+        out_shape=jax.ShapeDtypeStruct((bins, rows, width), bf16),
         in_specs=in_specs,
-        out_specs=pl.BlockSpec((1, step, weights.shape[2]), lambda i, h: (first + i, h, 0)),
+        out_specs=anywhere,
+        scratch_shapes=[
+            pltpu.VMEM(z.shape, bf16),
+            pltpu.VMEM((count, rows, width), bf16),
+            pltpu.SemaphoreType.DMA((count,)),
+            pltpu.SemaphoreType.DMA((count,)),
+        ],
         input_output_aliases=aliases,
-        compiler_params=params(),
+        compiler_params=params(63 if count > 3 else 32),
         name="beams",
     )(*operands)
 
@@ -380,12 +429,10 @@
         owned.append(lax.all_to_all(sent, "blk", split_axis=0, concat_axis=0, tiled=True))
     result = None
     for first, y in zip(firsts, owned):
-        if result is not None:
-            y, result = lax.optimization_barrier((y, result))
         cov = covariance(y, blocks, hard, first)
-        c3, c1, c2 = shifted(cov, 3), shifted(cov, 1), shifted(cov, 2)
+        c1, c3, twos = earlier(cov)
         z = compress(y, table)
-        weights = beam_weights(c1, c2, c3)
+        weights = beam_weights(c1, c3, twos)
         result = form_beams(z, weights, result, bins, first)
     return result[None]
 

time: 194 us -> 175 us (0.902)
  the two profiles are of different devices: /device:TPU:1 before, /device:TPU:0 now
where the time goes in v3:
time: 175 us
  waiting for transfers between devices  89.1 us (51%)
  Pallas kernels  52.6 us (30%)
  starting transfers between devices  24.5 us (14%)
  local copies, waits for them, and re-layouts  5.35 us (3%)
  matrix products  2.64 us (2%)
    all_to_all x2, waiting for transfers between devices, chain(): lax.all_to_all(sent, 'blk', split_axis=0, concat_axis=0, tiled=True)  80.5 us
    pallas_call x2, Pallas kernels, doppler(): pl.pallas_call(make_doppler_kernel(owners, first, count), out_shape=pltpu...  15.4 us
    pallas_call x2, Pallas kernels, beam_weights(): pl.pallas_call(weights_kernel, out_shape=jax.ShapeDtypeStruct((count, 2 *...  14.1 us
    all_to_all x2, starting transfers between devices, chain(): lax.all_to_all(sent, 'blk', split_axis=0, concat_axis=0, tiled=True)  12.4 us
    ppermute x7, starting transfers between devices, shifted(): lax.ppermute(x, 'segment', [(i, (i + by) % peers) for i in range(peers)])  12.1 us
    pallas_call x2, Pallas kernels, form_beams(): pl.pallas_call(make_beams_kernel(first), out_shape=jax.ShapeDtypeStruct((...  10.1 us
    ppermute x7, waiting for transfers between devices, shifted(): lax.ppermute(x, 'segment', [(i, (i + by) % peers) for i in range(peers)])  8.64 us
    pallas_call x2, Pallas kernels, compress(): pl.pallas_call(compress_kernel, out_shape=place((count, sources * per, wi...  8.49 us
  transfers between devices with their start and end apart: 9, of which 3 were waited for; matrix products, arithmetic and copies ran while one was open for 3% of the time, Pallas kernels for 20%

profile of v3, /device:TPU:0, one launch (start us, length us, event | category | flops | bytes accessed | tf_op | source)
XLA Modules:
  0.0 174.6 jit_solution(12748996043387092594)
XLA Ops:
  0.0 8.7 %doppler.3 = bf16[192,64,256]{2,1,0:T(8,128)(2,1)} custom-call(s32[1,256]{1,0:T(1,128)} %bitcast.25, bf16[64,128,512]{2,1,0:T(8,128)(2,1)} %bitcast.21), custom_call_target="tpu_custom_call" | custom-call | tf_op jit(solution)/shard_map/doppler/pallas_call | solution.py:122
  8.7 8.4 %all-to-all-start = ((bf16[32,6,64,256]{3,2,1,0:T(8,128)(2,1)}), bf16[32,6,64,256]{3,2,1,0:T(8,128)(2,1)}, u32[]{:S(2)}, u32[]{:S(2)}) async-start(bf16[32,6,64,256]{3,2,1,0:T(8,128)(2,1)} %bitcast.23), calls=%async_computation | async-start | bytes 12582912 | tf_op jit(solution)/shard_map/all_to_all | solution.py:429
  17.1 6.7 %doppler.2 = bf16[64,64,256]{2,1,0:T(8,128)(2,1)} custom-call(s32[1,256]{1,0:T(1,128)} %bitcast.26, bf16[64,128,512]{2,1,0:T(8,128)(2,1)} %bitcast.22), custom_call_target="tpu_custom_call" | custom-call | tf_op jit(solution)/shard_map/doppler/pallas_call | solution.py:122
  23.8 0.0 copy-start.5
  23.8 0.0 copy-start.4
  23.9 71.1 %all-to-all-done.y_ref.y_hbm = bf16[32,6,64,256]{3,2,1,0:T(8,128)(2,1)} async-done(((bf16[32,6,64,256]{3,2,1,0:T(8,128)(2,1)}), bf16[32,6,64,256]{3,2,1,0:T(8,128)(2,1)}, u32[]{:S(2)}, u32[]{:S(2)}) %all-to-all-start) | async-done | bytes 6291488 | tf_op jit(solution)/shard_map/all_to_all | solution.py:429
  95.0 4.0 %all-to-all-start.1 = ((bf16[32,2,64,256]{3,2,1,0:T(8,128)(2,1)}), bf16[32,2,64,256]{3,2,1,0:T(8,128)(2,1)S(1)}, u32[]{:S(2)}, u32[]{:S(2)}) async-start(bf16[32,2,64,256]{3,2,1,0:T(8,128)(2,1)} %bitcast.24), calls=%async_computation.1 | async-start | bytes 4194304 | tf_op jit(solution)/shard_map/all_to_all | solution.py:429
  99.0 0.8 copy.7
  99.8 0.7 copy-done.3
  100.4 2.5 %covariance.3 = f32[6,128,128]{2,1,0:T(8,128)S(1)} custom-call(s32[8,6]{1,0:T(8,128)S(1)} %bitcast.17, s32[8]{0:T(128)S(1)} %bitcast.19, bf16[32,6,64,256]{3,2,1,0:T(8,128)(2,1)} %all-to-all-done.y_ref.y_hbm), custom_call_target="tpu_custom_call" | custom-call | tf_op jit(solution)/shard_map/covariance/pallas_call | solution.py:187
  102.9 3.1 %collective-permute-start.4 = (f32[6,128,128]{2,1,0:T(8,128)S(1)}, f32[6,128,128]{2,1,0:T(8,128)S(1)}, u32[]{:S(2)}, u32[]{:S(2)}) collective-permute-start(f32[6,128,128]{2,1,0:T(8,128)S(1)} %covariance.3), channel_id=1, source_target_pairs={{0,96},{32,0},{64,32},{96,64},{1,97},{33,1},{65,33},{97,65},{2,98}... | collective-permute-start | bytes 1179656 | tf_op jit(solution)/shard_map/ppermute | solution.py:33
  106.0 0.0 collective-permute-start.3
  106.0 8.6 %collective-permute-done.4.c3_ref = f32[6,128,128]{2,1,0:T(8,128)S(1)} collective-permute-done((f32[6,128,128]{2,1,0:T(8,128)S(1)}, f32[6,128,128]{2,1,0:T(8,128)S(1)}, u32[]{:S(2)}, u32[]{:S(2)}) %collective-permute-start.4) | collective-permute-done | bytes 393248 | tf_op jit(solution)/shard_map/ppermute | solution.py:33
  114.7 0.7 slice.9
  115.4 3.7 %collective-permute-start.6 = (f32[3,128,128]{2,1,0:T(8,128)}, f32[3,128,128]{2,1,0:T(8,128)S(1)}, u32[]{:S(2)}, u32[]{:S(2)}) collective-permute-start(f32[3,128,128]{2,1,0:T(8,128)} %slice.9), channel_id=1, source_target_pairs={{0,96},{32,0},{64,32},{96,64},{1,97},{33,1},{65,33},{97,65},{2,98}... | collective-permute-start | bytes 589832 | tf_op jit(solution)/shard_map/ppermute | solution.py:33
  119.1 0.7 slice.8
  119.8 0.0 collective-permute-start.5
  119.8 9.4 %all-to-all-done.1.y_ref.y_hbm = bf16[32,2,64,256]{3,2,1,0:T(8,128)(2,1)S(1)} async-done(((bf16[32,2,64,256]{3,2,1,0:T(8,128)(2,1)}), bf16[32,2,64,256]{3,2,1,0:T(8,128)(2,1)S(1)}, u32[]{:S(2)}, u32[]{:S(2)}) %all-to-all-start.1) | async-done | bytes 2097184 | tf_op jit(solution)/shard_map/all_to_all | solution.py:429
  129.1 2.0 %covariance.2 = f32[2,128,128]{2,1,0:T(8,128)} custom-call(s32[8,6]{1,0:T(8,128)S(1)} %bitcast.18, s32[8]{0:T(128)S(1)} %bitcast.20, bf16[32,2,64,256]{3,2,1,0:T(8,128)(2,1)S(1)} %all-to-all-done.1.y_ref.y_hbm), custom_call_target="tpu_custom_call" | custom-call | tf_op jit(solution)/shard_map/covariance/pallas_call | solution.py:187
  131.2 3.3 %collective-permute-start.2 = (f32[2,128,128]{2,1,0:T(8,128)}, f32[2,128,128]{2,1,0:T(8,128)}, u32[]{:S(2)}, u32[]{:S(2)}) collective-permute-start(f32[2,128,128]{2,1,0:T(8,128)} %covariance.2), channel_id=1, source_target_pairs={{0,64},{32,96},{64,0},{96,32},{1,65},{33,97},{65,1},{97,33},{2,66}... | collective-permute-start | bytes 393224 | tf_op jit(solution)/shard_map/ppermute | solution.py:33
  134.4 1.1 collective-permute-start.1
  135.5 1.0 collective-permute-start
  136.5 2.6 %fusion.2 = bf16[2,128,256]{2,0,1:T(2,128)(2,1)S(1)} fusion(s32[128,256]{1,0:T(8,128)S(1)} %iota_subtract_fusion, f32[1,64]{1,0:T(1,128)S(1)} %get-tuple-element.14, f32[1,64]{1,0:T(1,128)S(1)} %get-tuple-element.13), kind=kOutput, calls=%fused_computation.3 | convolution fusion | flops 52494592 | bytes 262656 | tf_op jit(solution)/shard_map/pql,kl->kpq/dot_general | solution.py:311
  139.1 6.6 %compress.3.z_hbm = bf16[6,2048,256]{2,1,0:T(8,128)(2,1)} custom-call(bf16[256,256]{1,0:T(8,128)(2,1)S(1)} %bitcast.15, bf16[32,6,64,256]{3,2,1,0:T(8,128)(2,1)} %all-to-all-done.y_ref.y_hbm), custom_call_target="tpu_custom_call" | custom-call | tf_op jit(solution)/shard_map/compress/pallas_call | solution.py:346
  145.8 0.0 collective-permute-done.6.refs_1_
  145.8 8.1 %weights.3.w_ref = bf16[6,256,256]{2,1,0:T(8,128)(2,1)S(1)} custom-call(f32[6,128,128]{2,1,0:T(8,128)S(1)} %collective-permute-done.3.c1_ref, f32[6,128,128]{2,1,0:T(8,128)S(1)} %collective-permute-done.4.c3_ref, f32[3,128,128]{2,1,0:T(8,128)S(1)} %collective-permute-done.5.refs_0_, f32[3,128,128]{2,1,0:T(8,128)S(1)} %collective-permute-done.6.refs_1_), custom_call_target="tpu_custom_call" | custom-call | tf_op jit(solution)/shard_map/weights/pallas_call | solution.py:281
  153.9 0.9 copy-done.2
  154.8 7.6 %beams.2.refs_0_ = bf16[8,2048,256]{2,1,0:T(8,128)(2,1)} custom-call(bf16[6,256,256]{2,1,0:T(8,128)(2,1)} %copy-done.2, bf16[6,2048,256]{2,1,0:T(8,128)(2,1)} %compress.3.z_hbm), custom_call_target="tpu_custom_call" | custom-call | tf_op jit(solution)/shard_map/beams/pallas_call | solution.py:396
  162.4 1.6 copy-done.1
  164.0 1.9 %compress.2.z_hbm = bf16[2,2048,256]{2,1,0:T(8,128)(2,1)S(1)} custom-call(bf16[256,256]{1,0:T(8,128)(2,1)S(1)} %bitcast.16, bf16[32,2,64,256]{3,2,1,0:T(8,128)(2,1)S(1)} %copy-done.1), custom_call_target="tpu_custom_call" | custom-call | tf_op jit(solution)/shard_map/compress/pallas_call | solution.py:346
  165.9 6.0 %weights.2.w_ref = bf16[2,256,256]{2,1,0:T(8,128)(2,1)S(1)} custom-call(f32[2,128,128]{2,1,0:T(8,128)} %collective-permute-done.c1_ref, f32[2,128,128]{2,1,0:T(8,128)} %collective-permute-done.1.c3_ref, f32[2,128,128]{2,1,0:T(8,128)} %collective-permute-done.2.refs_0_), custom_call_target="tpu_custom_call" | custom-call | tf_op jit(solution)/shard_map/weights/pallas_call | solution.py:281
  171.9 2.5 %beams.3 = bf16[8,2048,256]{2,1,0:T(8,128)(2,1)} custom-call(bf16[2,256,256]{2,1,0:T(8,128)(2,1)S(1)} %weights.2.w_ref, bf16[2,2048,256]{2,1,0:T(8,128)(2,1)S(1)} %compress.2.z_hbm, bf16[8,2048,256]{2,1,0:T(8,128)(2,1)} %beams.2.refs_0_), custom_call_target="tpu_custom_call", output_to_operand_aliasing={{}: (2, {})} | custom-call | tf_op jit(solution)/shard_map/beams/pallas_call | solution.py:396
  (15 shorter events, 0.1 us)
Async XLA Ops:
  8.7 86.3 %all-to-all-start = ((bf16[32,6,64,256]{3,2,1,0:T(8,128)(2,1)}), bf16[32,6,64,256]{3,2,1,0:T(8,128)(2,1)}, u32[]{:S(2)}, u32[]{:S(2)}) async-start(bf16[32,6,64,256]{3,2,1,0:T(8,128)(2,1)} %bitcast.23), calls=%async_computation | async-start | bytes 12582912 | tf_op jit(solution)/shard_map/all_to_all | solution.py:429
  23.8 82.2 %copy-start.5 = (f32[64]{0:T(128)S(1)}, f32[64]{0:T(128)}, u32[]{:S(2)}) copy-start(f32[64]{0:T(128)} %param.9) | copy-start | bytes 772
  23.8 105.3 %copy-start.4 = (s32[1,8]{1,0:T(1,128)S(1)}, s32[1,8]{1,0:T(1,128)}, u32[]{:S(2)}) copy-start(s32[1,8]{1,0:T(1,128)} %param.7) | copy-start | bytes 100
  95.0 34.1 %all-to-all-start.1 = ((bf16[32,2,64,256]{3,2,1,0:T(8,128)(2,1)}), bf16[32,2,64,256]{3,2,1,0:T(8,128)(2,1)S(1)}, u32[]{:S(2)}, u32[]{:S(2)}) async-start(bf16[32,2,64,256]{3,2,1,0:T(8,128)(2,1)} %bitcast.24), calls=%async_computation.1 | async-start | bytes 4194304 | tf_op jit(solution)/shard_map/all_to_all | solution.py:429
  99.8 0.7 copy-start.3
  102.9 11.8 %collective-permute-start.4 = (f32[6,128,128]{2,1,0:T(8,128)S(1)}, f32[6,128,128]{2,1,0:T(8,128)S(1)}, u32[]{:S(2)}, u32[]{:S(2)}) collective-permute-start(f32[6,128,128]{2,1,0:T(8,128)S(1)} %covariance.3), channel_id=1, source_target_pairs={{0,96},{32,0},{64,32},{96,64},{1,97},{33,1},{65,33},{97,65},{2,98}... | collective-permute-start | bytes 1179656 | tf_op jit(solution)/shard_map/ppermute | solution.py:33
  106.0 13.1 %collective-permute-start.3 = (f32[6,128,128]{2,1,0:T(8,128)S(1)}, f32[6,128,128]{2,1,0:T(8,128)S(1)}, u32[]{:S(2)}, u32[]{:S(2)}) collective-permute-start(f32[6,128,128]{2,1,0:T(8,128)S(1)} %covariance.3), channel_id=1, source_target_pairs={{0,32},{32,64},{64,96},{96,0},{1,33},{33,65},{65,97},{97,1},{2,34}... | collective-permute-start | bytes 1179656 | tf_op jit(solution)/shard_map/ppermute | solution.py:33
  115.4 30.4 %collective-permute-start.6 = (f32[3,128,128]{2,1,0:T(8,128)}, f32[3,128,128]{2,1,0:T(8,128)S(1)}, u32[]{:S(2)}, u32[]{:S(2)}) collective-permute-start(f32[3,128,128]{2,1,0:T(8,128)} %slice.9), channel_id=1, source_target_pairs={{0,96},{32,0},{64,32},{96,64},{1,97},{33,1},{65,33},{97,65},{2,98}... | collective-permute-start | bytes 589832 | tf_op jit(solution)/shard_map/ppermute | solution.py:33
  119.8 26.1 %collective-permute-start.5 = (f32[3,128,128]{2,1,0:T(8,128)}, f32[3,128,128]{2,1,0:T(8,128)S(1)}, u32[]{:S(2)}, u32[]{:S(2)}) collective-permute-start(f32[3,128,128]{2,1,0:T(8,128)} %slice.8), channel_id=1, source_target_pairs={{0,32},{32,64},{64,96},{96,0},{1,33},{33,65},{65,97},{97,1},{2,34}... | collective-permute-start | bytes 589832 | tf_op jit(solution)/shard_map/ppermute | solution.py:33
  129.1 16.7 %copy-start = (bf16[32,2,64,256]{3,2,1,0:T(8,128)(2,1)}, bf16[32,2,64,256]{3,2,1,0:T(8,128)(2,1)S(1)}, u32[]{:S(2)}) copy-start(bf16[32,2,64,256]{3,2,1,0:T(8,128)(2,1)S(1)} %all-to-all-done.1.y_ref.y_hbm) | copy-start | bytes 6291460
  131.2 34.7 %collective-permute-start.2 = (f32[2,128,128]{2,1,0:T(8,128)}, f32[2,128,128]{2,1,0:T(8,128)}, u32[]{:S(2)}, u32[]{:S(2)}) collective-permute-start(f32[2,128,128]{2,1,0:T(8,128)} %covariance.2), channel_id=1, source_target_pairs={{0,64},{32,96},{64,0},{96,32},{1,65},{33,97},{65,1},{97,33},{2,66}... | collective-permute-start | bytes 393224 | tf_op jit(solution)/shard_map/ppermute | solution.py:33
  134.4 31.4 %collective-permute-start.1 = (f32[2,128,128]{2,1,0:T(8,128)}, f32[2,128,128]{2,1,0:T(8,128)}, u32[]{:S(2)}, u32[]{:S(2)}) collective-permute-start(f32[2,128,128]{2,1,0:T(8,128)} %covariance.2), channel_id=1, source_target_pairs={{0,96},{32,0},{64,32},{96,64},{1,97},{33,1},{65,33},{97,65},{2,98}... | collective-permute-start | bytes 393224 | tf_op jit(solution)/shard_map/ppermute | solution.py:33
  135.5 30.4 %collective-permute-start = (f32[2,128,128]{2,1,0:T(8,128)}, f32[2,128,128]{2,1,0:T(8,128)}, u32[]{:S(2)}, u32[]{:S(2)}) collective-permute-start(f32[2,128,128]{2,1,0:T(8,128)} %covariance.2), channel_id=1, source_target_pairs={{0,32},{32,64},{64,96},{96,0},{1,33},{33,65},{65,97},{97,1},{2,34}... | collective-permute-start | bytes 393224 | tf_op jit(solution)/shard_map/ppermute | solution.py:33
  153.9 0.9 copy-start.2
  162.4 1.6 copy-start.1
